TPU v7x, 32 devices: a whole 2x2x4 slice. The times are simulated.
32 devices in a mesh: rep: 1, ep: 32 (over z, y, x, core).
Axes of the slice: x: 2, y: 2, z: 4, core: 2. Of those that a mesh axis runs over, the one named last changes fastest.
Arguments:
- tokens: bfloat16 [512, 3584], P(('rep', 'ep')), may hold values from -6 to 6
- routes: int32 [512, 8], P(('rep', 'ep')), may hold values from 0 to 15, all different within a row; in each aligned block of 16 rows (0 to 15, 16 to 31, ...) at most 16 rows name the same one
- gate_weights: float32 [512, 8], P(('rep', 'ep')), may hold values from 0.05 to 0.5
- w_gate: bfloat16 [32, 3584, 512], P('ep'), may hold values from -0.09375 to 0.09375
- w_up: bfloat16 [32, 3584, 512], P('ep'), may hold values from -0.09375 to 0.09375
- w_down: bfloat16 [32, 512, 3584], P('ep'), may hold values from -0.1875 to 0.1875
Outputs:
- mixed: bfloat16 [512, 3584], P(('rep', 'ep'))
Inputs may be any that keep to these rules, and one draw needn't show every extreme that they name: `routes`: each token names 8 different experts. Among the tokens of one device at most 16 name any one expert, and in every draw some expert is named by exactly 16 tokens of some device.
All inputs are finite; a program needn't handle non-finite values.
Results may differ from a plain program's by a relative error of at most 0.008.
Values may be sent and summed in bfloat16 or wider, within the bound.
No kernel may reach another device: no remote copies, remote signals or barrier semaphores. Data moves between devices by JAX's collectives and lax.ppermute only.
A program may use at most 128 MiB of HBM per device.

v0:
```python
import functools

import jax
import jax.numpy as jnp
from jax import lax
from jax.experimental import pallas as pl
from jax.experimental.pallas import tpu as pltpu
from jax.sharding import PartitionSpec as P


RESIDENT, VMEM_MIB = 3, 20


def exchange(value, mask):
    pairs = [(source, source ^ mask) for source in range(lax.axis_size("ep"))]
    return lax.ppermute(value, "ep", pairs)


def tree_plan(bits):
    steps = []
    for hops in range(1, bits):
        chosen = {bit: [] for bit in range(bits)}
        for mask in range(1 << bits):
            if mask.bit_count() == hops:
                held = [bit for bit in range(bits) if mask >> bit & 1]
                bit = min(held, key=lambda candidate: len(chosen[candidate]))
                chosen[bit].append(mask)
        steps.append([(bit, masks) for bit, masks in chosen.items() if masks])
    return steps


def joined(parts):
    return parts[0] if len(parts) == 1 else jnp.concatenate(parts, axis=0)


def gather_tree(own, bits, last_bit):
    count = own.shape[0]
    held = {0: own}
    for step in tree_plan(bits):
        for bit, masks in step:
            arrived = exchange(joined([held[mask ^ (1 << bit)] for mask in masks]), 2 << bit)
            for place, mask in enumerate(masks):
                held[mask] = arrived[count * place : count * (place + 1)]
        masks = [mask for _, group in step for mask in group]
        held.update(zip(masks, lax.optimization_barrier([held[mask] for mask in masks])))
    last = (1 << bits) - 1
    held[last] = exchange(held[last ^ (1 << last_bit)], 2 << last_bit)
    return held


def gather_rows(tokens, columns, bits):
    far_tokens = exchange(tokens, 2 << bits)
    far_columns = exchange(columns, 2 << bits)
    near = gather_tree(jnp.concatenate([tokens, columns], axis=1), bits, 0)
    far = gather_tree(jnp.concatenate([far_tokens, far_columns], axis=1), bits, 1)
    return {mask: (near[mask], far[mask]) for mask in near}


def summed(parts):
    if len(parts) == 1:
        return parts[0]
    total = parts[0].astype(jnp.float32)
    for part in parts[1:]:
        total = total + part.astype(jnp.float32)
    return total.astype(parts[0].dtype)


def added(left, right):
    return summed([left, right])


def reduce_rows(held, bits):
    last = (1 << bits) - 1
    count = held[last].shape[0] // 2
    extra = {}
    for bit in range(2):
        rows = slice(bit * count, (bit + 1) * count)
        arrived = exchange(held[last][rows], 2 << bit)
        mask = last ^ (1 << bit)
        halves = [held[mask][:count], held[mask][count:]]
        halves[bit] = added(halves[bit], arrived)
        extra[mask] = jnp.concatenate(halves, axis=0)
    held = {**held, **extra}
    extra = {}
    steps = tree_plan(bits)
    for step in reversed(steps[1:]):
        for bit, masks in step:
            arrived = exchange(joined([held[mask] for mask in masks]), 2 << bit)
            for place, mask in enumerate(masks):
                piece = arrived[2 * count * place : 2 * count * (place + 1)]
                target = mask ^ (1 << bit)
                if target.bit_count() > 1:
                    held[target] = added(held[target], piece)
                else:
                    extra.setdefault(target, []).append(piece)

    def last_sum(rows):
        parts = [held[0][rows]]
        for bit in range(bits):
            sent = [held[1 << bit][rows]] + [piece[rows] for piece in extra.get(1 << bit, [])]
            parts.append(exchange(summed(sent), 2 << bit))
        return parts

    far = summed(last_sum(slice(count, None)))
    arrived = exchange(far, 2 << bits)
    return summed(last_sum(slice(0, count)) + [arrived])


def gate_columns(routes, gate_weights, expert_count):
    hits = routes[:, :, None] == jnp.arange(expert_count, dtype=jnp.int32)[None, None, :]
    left = jnp.sum(jnp.where(hits, gate_weights[:, :, None], 0.0), axis=1)
    pieces = []
    for _ in range(3):
        piece = lax.reduce_precision(left, 8, 7)
        pieces.append(piece.astype(jnp.bfloat16))
        left = left - piece
    columns = jnp.concatenate(pieces, axis=1)
    return jnp.pad(columns, ((0, 0), (0, -columns.shape[1] % 128)))


def load_kernel(*refs):
    sources, targets, sems = refs[:3], refs[3:6], refs[6]
    copies = [
        pltpu.make_async_copy(source, target, sems.at[place])
        for place, (source, target) in enumerate(zip(sources, targets))
    ]
    for copy in copies:
        copy.start()
    for copy in copies:
        copy.wait()


def load_weights(weights):
    weights = [pltpu.with_memory_space_constraint(value, pltpu.HBM) for value in weights]
    size = sum(2 * value.size for value in weights)
    return pl.pallas_call(
        load_kernel,
        out_shape=[jax.ShapeDtypeStruct(value.shape, value.dtype) for value in weights],
        in_specs=[pl.BlockSpec(memory_space=pltpu.HBM)] * 3,
        out_specs=[pl.BlockSpec(memory_space=pltpu.VMEM)] * 3,
        scratch_shapes=[pltpu.SemaphoreType.DMA((3,))],
        cost_estimate=pl.CostEstimate(flops=0, bytes_accessed=size, transcendentals=0),
        compiler_params=pltpu.CompilerParams(vmem_limit_bytes=2 * 1024 * 1024),
    )(*weights)


def expert_kernel(pieces, expert_count, width, chunk, splits, resident, *refs):
    piece_refs, weight_refs = refs[:pieces], list(refs[pieces : pieces + 6])
    out_refs = refs[pieces + 6 : pieces + 6 + pieces // 2]
    rows, hidden, *loaded = refs[pieces + 6 + pieces // 2 :]
    source_refs = weight_refs[resident:]
    weight_refs[resident:] = loaded[: 6 - resident]
    count = piece_refs[0].shape[0]
    depth = width // splits
    copies = [
        pltpu.make_async_copy(source, target, loaded[-1].at[place])
        for place, (source, target) in enumerate(zip(source_refs, weight_refs[resident:]))
    ]
    for copy in copies:
        copy.start()

    def ready(which):
        if which >= resident:
            copies[which - resident].wait()
        return weight_refs[which]

    expert = lax.div(lax.axis_index("ep"), 2)
    scales = []
    for place, piece_ref in enumerate(piece_refs):
        rows[place * count : (place + 1) * count, :] = piece_ref[:, :width]
        columns = piece_ref[:, width:].astype(jnp.float32)
        lane = lax.broadcasted_iota(jnp.int32, columns.shape, 1)
        mine = (lax.rem(lane, expert_count) == expert) & (lane < 3 * expert_count)
        scales.append(jnp.sum(jnp.where(mine, columns, 0.0), axis=1, keepdims=True))
    for half in range(2):
        totals = []
        for kind in range(2):
            weight_ref, total = ready(3 * half + kind), 0.0
            for part in range(splits):
                inner = slice(part * depth, (part + 1) * depth)
                total += jnp.dot(
                    rows[:, inner], weight_ref[inner, :], preferred_element_type=jnp.float32
                )
            totals.append(total)
        hidden[half] = (jax.nn.silu(totals[0]) * totals[1]).astype(jnp.bfloat16)
        ready(3 * half + 2)
    for start in range(0, width, chunk):
        cols = slice(start, start + chunk)
        value = jnp.dot(hidden[0], weight_refs[2][:, cols], preferred_element_type=jnp.float32)
        value += jnp.dot(hidden[1], weight_refs[5][:, cols], preferred_element_type=jnp.float32)
        for place, scale in enumerate(scales):
            piece = value[place * count : (place + 1) * count] * scale
            target = slice(place % 2 * count, (place % 2 + 1) * count)
            out_refs[place // 2][target, cols] = piece.astype(jnp.bfloat16)


def run_expert(pieces, weights, expert_count):
    count = pieces[0].shape[0]
    units, width = weights[2].shape
    vmem, hbm = pl.BlockSpec(memory_space=pltpu.VMEM), pl.BlockSpec(memory_space=pltpu.HBM)
    rows = count * len(pieces)
    chunk, splits, resident = 512, 2, RESIDENT
    scratch = [
        pltpu.VMEM((rows, width), jnp.bfloat16),
        pltpu.VMEM((2, rows, units), jnp.bfloat16),
    ]
    scratch += [pltpu.VMEM(value.shape, value.dtype) for value in weights[resident:]]
    if resident < 6:
        scratch.append(pltpu.SemaphoreType.DMA((6 - resident,)))
    weights = weights[:resident] + tuple(
        pltpu.with_memory_space_constraint(value, pltpu.HBM) for value in weights[resident:]
    )
    return pl.pallas_call(
        functools.partial(expert_kernel, len(pieces), expert_count, width, chunk, splits, resident),
        out_shape=[jax.ShapeDtypeStruct((2 * count, width), jnp.bfloat16)] * (len(pieces) // 2),
        in_specs=[vmem] * (len(pieces) + resident) + [hbm] * (6 - resident),
        out_specs=[vmem] * (len(pieces) // 2),
        scratch_shapes=scratch,
        cost_estimate=pl.CostEstimate(
            flops=12 * rows * width * units,
            bytes_accessed=12 * width * units + 4 * rows * width,
            transcendentals=2 * rows * units,
        ),
        compiler_params=pltpu.CompilerParams(vmem_limit_bytes=VMEM_MIB * 1024 * 1024),
    )(*pieces, *weights)


def body(tokens, routes, gate_weights, w_gate, w_up, w_down):
    devices = lax.axis_size("ep")
    expert_count = devices // 2
    bits = expert_count.bit_length() - 2
    weights = (w_gate[0], w_up[0], w_down[0])
    swapped = tuple(exchange(value, 1) for value in weights)
    own = load_weights(weights)
    columns = gate_columns(routes, gate_weights, expert_count)
    held = gather_rows(tokens, columns, bits)
    order = sorted(held, key=lambda mask: mask.bit_count())
    pieces = [piece for mask in order for piece in held[mask]]
    sums = run_expert(pieces, tuple(own) + swapped, expert_count)
    return reduce_rows(dict(zip(order, sums)), bits)


def solution(mesh):
    placed = (
        P(("rep", "ep"), None),
        P(("rep", "ep"), None),
        P(("rep", "ep"), None),
        P("ep", None, None),
        P("ep", None, None),
        P("ep", None, None),
    )
    return jax.shard_map(
        body, mesh=mesh, in_specs=placed, out_specs=P(("rep", "ep"), None), check_vma=False
    )
```

profile of v0, /device:TPU:0, one launch (start us, length us, event | category | flops | bytes accessed | tf_op | source)
XLA Modules:
  0.0 86.2 jit_solution(12929435630078681822)
XLA Ops:
  2.7 3.6 %collective-permute-start.1 = (bf16[16,128]{1,0:T(8,128)(2,1)S(1)}, bf16[16,128]{1,0:T(8,128)(2,1)S(1)}, u32[]{:S(2)}, u32[]{:S(2)}) collective-permute-start(bf16[16,128]{1,0:T(8,128)(2,1)S(1)} %fusion.6), channel_id=1, source_target_pairs={{0,16},{1,17},{2,18},{3,19},{4,20},{5,21},{6,22},{7,23},{8,24},{9,... | collective-permute-start | bytes 12296 | tf_op jit(solution)/shard_map/ppermute | solution.py:16
  6.4 0.9 %pad_maximum_fusion.2.refs_0_ = bf16[16,3712]{1,0:T(8,128)(2,1)S(1)} fusion(bf16[16,128]{1,0:T(8,128)(2,1)S(1)} %fusion.6, bf16[16,3584]{1,0:T(8,128)(2,1)} %param.6), kind=kLoop, calls=%fused_computation.12 | loop fusion | flops 237568 | bytes 237568 | tf_op jit(solution)/shard_map/concatenate | solution.py:54
  7.9 1.9 %collective-permute-start.4 = (bf16[16,3712]{1,0:T(8,128)(2,1)S(1)}, bf16[16,3712]{1,0:T(8,128)(2,1)S(1)}, u32[]{:S(2)}, u32[]{:S(2)}) collective-permute-start(bf16[16,3712]{1,0:T(8,128)(2,1)S(1)} %pad_maximum_fusion.2.refs_0_), channel_id=1, source_target_pairs={{0,8},{1,9},{2,10},{3,11},{4,12},{5,13},{6,14},{7,15},{8,0},{9,1},... | collective-permute-start | bytes 356360 | tf_op jit(solution)/shard_map/ppermute | solution.py:16
  9.8 5.4 %collective-permute-done = bf16[16,3584]{1,0:T(8,128)(2,1)S(1)} collective-permute-done((bf16[16,3584]{1,0:T(8,128)(2,1)}, bf16[16,3584]{1,0:T(8,128)(2,1)S(1)}, u32[]{:S(2)}, u32[]{:S(2)}) %collective-permute-start) | collective-permute-done | bytes 114720 | tf_op jit(solution)/shard_map/ppermute | solution.py:16
  15.2 1.5 %collective-permute-start.3 = (bf16[16,3712]{1,0:T(8,128)(2,1)S(1)}, bf16[16,3712]{1,0:T(8,128)(2,1)S(1)}, u32[]{:S(2)}, u32[]{:S(2)}) collective-permute-start(bf16[16,3712]{1,0:T(8,128)(2,1)S(1)} %pad_maximum_fusion.2.refs_0_), channel_id=1, source_target_pairs={{0,4},{1,5},{2,6},{3,7},{4,0},{5,1},{6,2},{7,3},{8,12},{9,13},{10,... | collective-permute-start | bytes 356360 | tf_op jit(solution)/shard_map/ppermute | solution.py:16
  16.8 1.6 %collective-permute-start.2 = (bf16[16,3712]{1,0:T(8,128)(2,1)S(1)}, bf16[16,3712]{1,0:T(8,128)(2,1)S(1)}, u32[]{:S(2)}, u32[]{:S(2)}) collective-permute-start(bf16[16,3712]{1,0:T(8,128)(2,1)S(1)} %pad_maximum_fusion.2.refs_0_), channel_id=1, source_target_pairs={{0,2},{1,3},{2,0},{3,1},{4,6},{5,7},{6,4},{7,5},{8,10},{9,11},{10,... | collective-permute-start | bytes 356360 | tf_op jit(solution)/shard_map/ppermute | solution.py:16
  18.3 1.7 %collective-permute-done.3.refs_4_ = bf16[16,3712]{1,0:T(8,128)(2,1)S(1)} collective-permute-done((bf16[16,3712]{1,0:T(8,128)(2,1)S(1)}, bf16[16,3712]{1,0:T(8,128)(2,1)S(1)}, u32[]{:S(2)}, u32[]{:S(2)}) %collective-permute-start.3) | collective-permute-done | bytes 118816 | tf_op jit(solution)/shard_map/ppermute | solution.py:16
  20.1 1.6 %collective-permute-done.2.refs_2_ = bf16[16,3712]{1,0:T(8,128)(2,1)S(1)} collective-permute-done((bf16[16,3712]{1,0:T(8,128)(2,1)S(1)}, bf16[16,3712]{1,0:T(8,128)(2,1)S(1)}, u32[]{:S(2)}, u32[]{:S(2)}) %collective-permute-start.2) | collective-permute-done | bytes 118816 | tf_op jit(solution)/shard_map/ppermute | solution.py:16
  22.2 2.7 %collective-permute-done.7.refs_7_ = bf16[16,3712]{1,0:T(8,128)(2,1)S(1)} collective-permute-done((bf16[16,3712]{1,0:T(8,128)(2,1)S(1)}, bf16[16,3712]{1,0:T(8,128)(2,1)S(1)}, u32[]{:S(2)}, u32[]{:S(2)}) %collective-permute-start.7) | collective-permute-done | bytes 118816 | tf_op jit(solution)/shard_map/ppermute | solution.py:16
  24.9 1.5 %collective-permute-start.5 = (bf16[16,3712]{1,0:T(8,128)(2,1)S(1)}, bf16[16,3712]{1,0:T(8,128)(2,1)S(1)}, u32[]{:S(2)}, u32[]{:S(2)}) collective-permute-start(bf16[16,3712]{1,0:T(8,128)(2,1)S(1)} %constant_dynamic-update-slice_fusion.refs_1_), channel_id=1, source_target_pairs={{0,2},{1,3},{2,0},{3,1},{4,6},{5,7},{6,4},{7,5},{8,10},{9,11},{10,... | collective-permute-start | bytes 356360 | tf_op jit(solution)/shard_map/ppermute | solution.py:16
  26.9 4.1 %collective-permute-done.5.refs_3_ = bf16[16,3712]{1,0:T(8,128)(2,1)S(1)} collective-permute-done((bf16[16,3712]{1,0:T(8,128)(2,1)S(1)}, bf16[16,3712]{1,0:T(8,128)(2,1)S(1)}, u32[]{:S(2)}, u32[]{:S(2)}) %collective-permute-start.5) | collective-permute-done | bytes 118816 | tf_op jit(solution)/shard_map/ppermute | solution.py:16
  31.0 1.5 %collective-permute-start.8 = (bf16[16,3712]{1,0:T(8,128)(2,1)S(1)}, bf16[16,3712]{1,0:T(8,128)(2,1)S(1)}, u32[]{:S(2)}, u32[]{:S(2)}) collective-permute-start(bf16[16,3712]{1,0:T(8,128)(2,1)S(1)} %collective-permute-done.3.refs_4_), channel_id=1, source_target_pairs={{0,2},{1,3},{2,0},{3,1},{4,6},{5,7},{6,4},{7,5},{8,10},{9,11},{10,... | collective-permute-start | bytes 356360 | tf_op jit(solution)/shard_map/ppermute | solution.py:16
  32.5 1.3 %collective-permute-start.9 = (bf16[16,3712]{1,0:T(8,128)(2,1)S(1)}, bf16[16,3712]{1,0:T(8,128)(2,1)S(1)}, u32[]{:S(2)}, u32[]{:S(2)}) collective-permute-start(bf16[16,3712]{1,0:T(8,128)(2,1)S(1)} %collective-permute-done.4.refs_6_), channel_id=1, source_target_pairs={{0,4},{1,5},{2,6},{3,7},{4,0},{5,1},{6,2},{7,3},{8,12},{9,13},{10,... | collective-permute-start | bytes 356360 | tf_op jit(solution)/shard_map/ppermute | solution.py:16
  33.8 2.8 %collective-permute-done.8.refs_8_ = bf16[16,3712]{1,0:T(8,128)(2,1)S(1)} collective-permute-done((bf16[16,3712]{1,0:T(8,128)(2,1)S(1)}, bf16[16,3712]{1,0:T(8,128)(2,1)S(1)}, u32[]{:S(2)}, u32[]{:S(2)}) %collective-permute-start.8) | collective-permute-done | bytes 118816 | tf_op jit(solution)/shard_map/ppermute | solution.py:16
  38.1 3.3 %collective-permute-done.13.refs_13_ = bf16[16,3712]{1,0:T(8,128)(2,1)S(1)} collective-permute-done((bf16[16,3712]{1,0:T(8,128)(2,1)S(1)}, bf16[16,3712]{1,0:T(8,128)(2,1)S(1)}, u32[]{:S(2)}, u32[]{:S(2)}) %collective-permute-start.13) | collective-permute-done | bytes 118816 | tf_op jit(solution)/shard_map/ppermute | solution.py:16
  41.4 0.9 %collective-permute-start.12 = (bf16[16,3712]{1,0:T(8,128)(2,1)S(1)}, bf16[16,3712]{1,0:T(8,128)(2,1)S(1)}, u32[]{:S(2)}, u32[]{:S(2)}) collective-permute-start(bf16[16,3712]{1,0:T(8,128)(2,1)S(1)} %collective-permute-done.7.refs_7_), channel_id=1, source_target_pairs={{0,4},{1,5},{2,6},{3,7},{4,0},{5,1},{6,2},{7,3},{8,12},{9,13},{10,... | collective-permute-start | bytes 356360 | tf_op jit(solution)/shard_map/ppermute | solution.py:16
  42.4 1.5 %collective-permute-start.14 = (bf16[16,3712]{1,0:T(8,128)(2,1)S(1)}, bf16[16,3712]{1,0:T(8,128)(2,1)S(1)}, u32[]{:S(2)}, u32[]{:S(2)}) collective-permute-start(bf16[16,3712]{1,0:T(8,128)(2,1)S(1)} %collective-permute-done.9.refs_10_), channel_id=1, source_target_pairs={{0,2},{1,3},{2,0},{3,1},{4,6},{5,7},{6,4},{7,5},{8,10},{9,11},{10,... | collective-permute-start | bytes 356360 | tf_op jit(solution)/shard_map/ppermute | solution.py:16
  43.8 2.4 %collective-permute-done.12.refs_11_ = bf16[16,3712]{1,0:T(8,128)(2,1)S(1)} collective-permute-done((bf16[16,3712]{1,0:T(8,128)(2,1)S(1)}, bf16[16,3712]{1,0:T(8,128)(2,1)S(1)}, u32[]{:S(2)}, u32[]{:S(2)}) %collective-permute-start.12) | collective-permute-done | bytes 118816 | tf_op jit(solution)/shard_map/ppermute | solution.py:16
  47.2 4.2 %shard_map.64 = (bf16[3584,512]{1,0:T(8,128)(2,1)S(1)}, bf16[3584,512]{1,0:T(8,128)(2,1)S(1)}, bf16[512,3584]{1,0:T(8,128)(2,1)S(1)}) custom-call(bf16[3584,512]{1,0:T(8,128)(2,1)} %bitcast.4, bf16[3584,512]{1,0:T(8,128)(2,1)} %bitcast.6, bf16[512,3584]{1,0:T(8,128)(2,1)} %bitcast.8), custom_call_target="tpu_custom_call" | custom-call | bytes 11010048 | tf_op jit(solution)/shard_map/pallas_call | solution.py:136
  51.5 8.3 %shard_map.65 = (bf16[32,3584]{1,0:T(8,128)(2,1)S(1)}, bf16[32,3584]{1,0:T(8,128)(2,1)S(1)}, bf16[32,3584]{1,0:T(8,128)(2,1)S(1)}, bf16[32,3584]{1,0:T(8,128)(2,...) custom-call(bf16[16,3712]{1,0:T(8,128)(2,1)S(1)} %pad_maximum_fusion, ...), custom_call_target="tpu_custom_call" | custom-call | flops 5637144576 | bytes 25690112 | tf_op jit(solution)/shard_map/pallas_call | solution.py:213
  59.8 1.6 %collective-permute-start.24 = (bf16[16,3584]{1,0:T(8,128)(2,1)S(1)}, bf16[16,3584]{1,0:T(8,128)(2,1)S(1)}, u32[]{:S(2)}, u32[]{:S(2)}) collective-permute-start(bf16[16,3584]{1,0:T(8,128)(2,1)S(1)} %get-tuple-element.58), channel_id=1, source_target_pairs={{0,2},{1,3},{2,0},{3,1},{4,6},{5,7},{6,4},{7,5},{8,10},{9,11},{10,... | collective-permute-start | bytes 344072 | tf_op jit(solution)/shard_map/ppermute | solution.py:16
  61.4 1.2 %collective-permute-start.19 = (bf16[16,3584]{1,0:T(8,128)(2,1)S(1)}, bf16[16,3584]{1,0:T(8,128)(2,1)S(1)}, u32[]{:S(2)}, u32[]{:S(2)}) collective-permute-start(bf16[16,3584]{1,0:T(8,128)(2,1)S(1)} %get-tuple-element.57), channel_id=1, source_target_pairs={{0,4},{1,5},{2,6},{3,7},{4,0},{5,1},{6,2},{7,3},{8,12},{9,13},{10,... | collective-permute-start | bytes 344072 | tf_op jit(solution)/shard_map/ppermute | solution.py:16
  63.1 1.6 %collective-permute-done.24 = bf16[16,3584]{1,0:T(8,128)(2,1)S(1)} collective-permute-done((bf16[16,3584]{1,0:T(8,128)(2,1)S(1)}, bf16[16,3584]{1,0:T(8,128)(2,1)S(1)}, u32[]{:S(2)}, u32[]{:S(2)}) %collective-permute-start.24) | collective-permute-done | bytes 114720 | tf_op jit(solution)/shard_map/ppermute | solution.py:16
  64.8 1.2 %collective-permute-start.25 = (bf16[32,3584]{1,0:T(8,128)(2,1)S(1)}, bf16[32,3584]{1,0:T(8,128)(2,1)S(1)}, u32[]{:S(2)}, u32[]{:S(2)}) collective-permute-start(bf16[32,3584]{1,0:T(8,128)(2,1)S(1)} %pad_maximum_fusion.1), channel_id=1, source_target_pairs={{0,4},{1,5},{2,6},{3,7},{4,0},{5,1},{6,2},{7,3},{8,12},{9,13},{10,... | collective-permute-start | bytes 688136 | tf_op jit(solution)/shard_map/ppermute | solution.py:16
  65.9 0.9 %collective-permute-done.19 = bf16[16,3584]{1,0:T(8,128)(2,1)S(1)} collective-permute-done((bf16[16,3584]{1,0:T(8,128)(2,1)S(1)}, bf16[16,3584]{1,0:T(8,128)(2,1)S(1)}, u32[]{:S(2)}, u32[]{:S(2)}) %collective-permute-start.19) | collective-permute-done | bytes 114720 | tf_op jit(solution)/shard_map/ppermute | solution.py:16
  67.0 2.8 %collective-permute-done.22 = bf16[32,3584]{1,0:T(8,128)(2,1)S(1)} collective-permute-done((bf16[32,3584]{1,0:T(8,128)(2,1)S(1)}, bf16[32,3584]{1,0:T(8,128)(2,1)S(1)}, u32[]{:S(2)}, u32[]{:S(2)}) %collective-permute-start.22) | collective-permute-done | bytes 229408 | tf_op jit(solution)/shard_map/ppermute | solution.py:16
  69.9 1.1 %collective-permute-start.28 = (bf16[16,3584]{1,0:T(8,128)(2,1)S(1)}, bf16[16,3584]{1,0:T(8,128)(2,1)S(1)}, u32[]{:S(2)}, u32[]{:S(2)}) collective-permute-start(bf16[16,3584]{1,0:T(8,128)(2,1)S(1)} %get-tuple-element.54), channel_id=1, source_target_pairs={{0,4},{1,5},{2,6},{3,7},{4,0},{5,1},{6,2},{7,3},{8,12},{9,13},{10,... | collective-permute-start | bytes 344072 | tf_op jit(solution)/shard_map/ppermute | solution.py:16
  71.5 2.1 %collective-permute-done.20 = bf16[32,3584]{1,0:T(8,128)(2,1)S(1)} collective-permute-done((bf16[32,3584]{1,0:T(8,128)(2,1)S(1)}, bf16[32,3584]{1,0:T(8,128)(2,1)S(1)}, u32[]{:S(2)}, u32[]{:S(2)}) %collective-permute-start.20) | collective-permute-done | bytes 229408 | tf_op jit(solution)/shard_map/ppermute | solution.py:16
  73.6 1.7 %collective-permute-start.27 = (bf16[16,3584]{1,0:T(8,128)(2,1)S(1)}, bf16[16,3584]{1,0:T(8,128)(2,1)S(1)}, u32[]{:S(2)}, u32[]{:S(2)}) collective-permute-start(bf16[16,3584]{1,0:T(8,128)(2,1)S(1)} %get-tuple-element.52), channel_id=1, source_target_pairs={{0,2},{1,3},{2,0},{3,1},{4,6},{5,7},{6,4},{7,5},{8,10},{9,11},{10,... | collective-permute-start | bytes 344072 | tf_op jit(solution)/shard_map/ppermute | solution.py:16
  76.1 1.6 %collective-permute-start.21 = (bf16[16,3584]{1,0:T(8,128)(2,1)S(1)}, bf16[16,3584]{1,0:T(8,128)(2,1)S(1)}, u32[]{:S(2)}, u32[]{:S(2)}) collective-permute-start(bf16[16,3584]{1,0:T(8,128)(2,1)S(1)} %get-tuple-element.51), channel_id=1, source_target_pairs={{0,2},{1,3},{2,0},{3,1},{4,6},{5,7},{6,4},{7,5},{8,10},{9,11},{10,... | collective-permute-start | bytes 344072 | tf_op jit(solution)/shard_map/ppermute | solution.py:16
  78.6 1.5 %collective-permute-done.23 = bf16[16,3584]{1,0:T(8,128)(2,1)S(1)} collective-permute-done((bf16[16,3584]{1,0:T(8,128)(2,1)S(1)}, bf16[16,3584]{1,0:T(8,128)(2,1)S(1)}, u32[]{:S(2)}, u32[]{:S(2)}) %collective-permute-start.23) | collective-permute-done | bytes 114720 | tf_op jit(solution)/shard_map/ppermute | solution.py:16
  80.9 4.6 %collective-permute-done.30 = bf16[16,3584]{1,0:T(8,128)(2,1)S(1)} collective-permute-done((bf16[16,3584]{1,0:T(8,128)(2,1)S(1)}, bf16[16,3584]{1,0:T(8,128)(2,1)S(1)}, u32[]{:S(2)}, u32[]{:S(2)}) %collective-permute-start.30) | collective-permute-done | bytes 114720 | tf_op jit(solution)/shard_map/ppermute | solution.py:16
  (52 shorter events, 11.4 us)
Async XLA Ops:
  0.0 51.4 %collective-permute-start.16 = (bf16[3584,512]{1,0:T(8,128)(2,1)}, bf16[3584,512]{1,0:T(8,128)(2,1)}, u32[]{:S(2)}, u32[]{:S(2)}) collective-permute-start(bf16[3584,512]{1,0:T(8,128)(2,1)} %bitcast.3), channel_id=1, source_target_pairs={{0,1},{1,0},{2,3},{3,2},{4,5},{5,4},{6,7},{7,6},{8,9},{9,8},{10,11... | collective-permute-start | bytes 11010056 | tf_op jit(solution)/shard_map/ppermute | solution.py:16
  0.5 51.0 %collective-permute-start.17 = (bf16[3584,512]{1,0:T(8,128)(2,1)}, bf16[3584,512]{1,0:T(8,128)(2,1)}, u32[]{:S(2)}, u32[]{:S(2)}) collective-permute-start(bf16[3584,512]{1,0:T(8,128)(2,1)} %bitcast.5), channel_id=1, source_target_pairs={{0,1},{1,0},{2,3},{3,2},{4,5},{5,4},{6,7},{7,6},{8,9},{9,8},{10,11... | collective-permute-start | bytes 11010056 | tf_op jit(solution)/shard_map/ppermute | solution.py:16
  0.5 51.0 %collective-permute-start.18 = (bf16[512,3584]{1,0:T(8,128)(2,1)}, bf16[512,3584]{1,0:T(8,128)(2,1)}, u32[]{:S(2)}, u32[]{:S(2)}) collective-permute-start(bf16[512,3584]{1,0:T(8,128)(2,1)} %bitcast.7), channel_id=1, source_target_pairs={{0,1},{1,0},{2,3},{3,2},{4,5},{5,4},{6,7},{7,6},{8,9},{9,8},{10,11... | collective-permute-start | bytes 11010056 | tf_op jit(solution)/shard_map/ppermute | solution.py:16
  2.7 5.2 %collective-permute-start.1 = (bf16[16,128]{1,0:T(8,128)(2,1)S(1)}, bf16[16,128]{1,0:T(8,128)(2,1)S(1)}, u32[]{:S(2)}, u32[]{:S(2)}) collective-permute-start(bf16[16,128]{1,0:T(8,128)(2,1)S(1)} %fusion.6), channel_id=1, source_target_pairs={{0,16},{1,17},{2,18},{3,19},{4,20},{5,21},{6,22},{7,23},{8,24},{9,... | collective-permute-start | bytes 12296 | tf_op jit(solution)/shard_map/ppermute | solution.py:16
  6.3 8.9 %collective-permute-start = (bf16[16,3584]{1,0:T(8,128)(2,1)}, bf16[16,3584]{1,0:T(8,128)(2,1)S(1)}, u32[]{:S(2)}, u32[]{:S(2)}) collective-permute-start(bf16[16,3584]{1,0:T(8,128)(2,1)} %param.6), channel_id=1, source_target_pairs={{0,16},{1,17},{2,18},{3,19},{4,20},{5,21},{6,22},{7,23},{8,24},{9,... | collective-permute-start | bytes 344072 | tf_op jit(solution)/shard_map/ppermute | solution.py:16
  7.9 8.9 %collective-permute-start.4 = (bf16[16,3712]{1,0:T(8,128)(2,1)S(1)}, bf16[16,3712]{1,0:T(8,128)(2,1)S(1)}, u32[]{:S(2)}, u32[]{:S(2)}) collective-permute-start(bf16[16,3712]{1,0:T(8,128)(2,1)S(1)} %pad_maximum_fusion.2.refs_0_), channel_id=1, source_target_pairs={{0,8},{1,9},{2,10},{3,11},{4,12},{5,13},{6,14},{7,15},{8,0},{9,1},... | collective-permute-start | bytes 356360 | tf_op jit(solution)/shard_map/ppermute | solution.py:16
  15.2 4.8 %collective-permute-start.3 = (bf16[16,3712]{1,0:T(8,128)(2,1)S(1)}, bf16[16,3712]{1,0:T(8,128)(2,1)S(1)}, u32[]{:S(2)}, u32[]{:S(2)}) collective-permute-start(bf16[16,3712]{1,0:T(8,128)(2,1)S(1)} %pad_maximum_fusion.2.refs_0_), channel_id=1, source_target_pairs={{0,4},{1,5},{2,6},{3,7},{4,0},{5,1},{6,2},{7,3},{8,12},{9,13},{10,... | collective-permute-start | bytes 356360 | tf_op jit(solution)/shard_map/ppermute | solution.py:16
  16.8 4.9 %collective-permute-start.2 = (bf16[16,3712]{1,0:T(8,128)(2,1)S(1)}, bf16[16,3712]{1,0:T(8,128)(2,1)S(1)}, u32[]{:S(2)}, u32[]{:S(2)}) collective-permute-start(bf16[16,3712]{1,0:T(8,128)(2,1)S(1)} %pad_maximum_fusion.2.refs_0_), channel_id=1, source_target_pairs={{0,2},{1,3},{2,0},{3,1},{4,6},{5,7},{6,4},{7,5},{8,10},{9,11},{10,... | collective-permute-start | bytes 356360 | tf_op jit(solution)/shard_map/ppermute | solution.py:16
  20.1 4.8 %collective-permute-start.7 = (bf16[16,3712]{1,0:T(8,128)(2,1)S(1)}, bf16[16,3712]{1,0:T(8,128)(2,1)S(1)}, u32[]{:S(2)}, u32[]{:S(2)}) collective-permute-start(bf16[16,3712]{1,0:T(8,128)(2,1)S(1)} %constant_dynamic-update-slice_fusion.refs_1_), channel_id=1, source_target_pairs={{0,8},{1,9},{2,10},{3,11},{4,12},{5,13},{6,14},{7,15},{8,0},{9,1},... | collective-permute-start | bytes 356360 | tf_op jit(solution)/shard_map/ppermute | solution.py:16
  21.7 4.8 %collective-permute-start.6 = (bf16[16,3712]{1,0:T(8,128)(2,1)S(1)}, bf16[16,3712]{1,0:T(8,128)(2,1)S(1)}, u32[]{:S(2)}, u32[]{:S(2)}) collective-permute-start(bf16[16,3712]{1,0:T(8,128)(2,1)S(1)} %constant_dynamic-update-slice_fusion.refs_1_), channel_id=1, source_target_pairs={{0,4},{1,5},{2,6},{3,7},{4,0},{5,1},{6,2},{7,3},{8,12},{9,13},{10,... | collective-permute-start | bytes 356360 | tf_op jit(solution)/shard_map/ppermute | solution.py:16
  24.9 6.1 %collective-permute-start.5 = (bf16[16,3712]{1,0:T(8,128)(2,1)S(1)}, bf16[16,3712]{1,0:T(8,128)(2,1)S(1)}, u32[]{:S(2)}, u32[]{:S(2)}) collective-permute-start(bf16[16,3712]{1,0:T(8,128)(2,1)S(1)} %constant_dynamic-update-slice_fusion.refs_1_), channel_id=1, source_target_pairs={{0,2},{1,3},{2,0},{3,1},{4,6},{5,7},{6,4},{7,5},{8,10},{9,11},{10,... | collective-permute-start | bytes 356360 | tf_op jit(solution)/shard_map/ppermute | solution.py:16
  26.5 6.0 %collective-permute-start.10 = (bf16[16,3712]{1,0:T(8,128)(2,1)S(1)}, bf16[16,3712]{1,0:T(8,128)(2,1)S(1)}, u32[]{:S(2)}, u32[]{:S(2)}) collective-permute-start(bf16[16,3712]{1,0:T(8,128)(2,1)S(1)} %collective-permute-done.2.refs_2_), channel_id=1, source_target_pairs={{0,8},{1,9},{2,10},{3,11},{4,12},{5,13},{6,14},{7,15},{8,0},{9,1},... | collective-permute-start | bytes 356360 | tf_op jit(solution)/shard_map/ppermute | solution.py:16
  31.0 5.6 %collective-permute-start.8 = (bf16[16,3712]{1,0:T(8,128)(2,1)S(1)}, bf16[16,3712]{1,0:T(8,128)(2,1)S(1)}, u32[]{:S(2)}, u32[]{:S(2)}) collective-permute-start(bf16[16,3712]{1,0:T(8,128)(2,1)S(1)} %collective-permute-done.3.refs_4_), channel_id=1, source_target_pairs={{0,2},{1,3},{2,0},{3,1},{4,6},{5,7},{6,4},{7,5},{8,10},{9,11},{10,... | collective-permute-start | bytes 356360 | tf_op jit(solution)/shard_map/ppermute | solution.py:16
  32.5 4.8 %collective-permute-start.9 = (bf16[16,3712]{1,0:T(8,128)(2,1)S(1)}, bf16[16,3712]{1,0:T(8,128)(2,1)S(1)}, u32[]{:S(2)}, u32[]{:S(2)}) collective-permute-start(bf16[16,3712]{1,0:T(8,128)(2,1)S(1)} %collective-permute-done.4.refs_6_), channel_id=1, source_target_pairs={{0,4},{1,5},{2,6},{3,7},{4,0},{5,1},{6,2},{7,3},{8,12},{9,13},{10,... | collective-permute-start | bytes 356360 | tf_op jit(solution)/shard_map/ppermute | solution.py:16
  36.6 4.8 %collective-permute-start.13 = (bf16[16,3712]{1,0:T(8,128)(2,1)S(1)}, bf16[16,3712]{1,0:T(8,128)(2,1)S(1)}, u32[]{:S(2)}, u32[]{:S(2)}) collective-permute-start(bf16[16,3712]{1,0:T(8,128)(2,1)S(1)} %collective-permute-done.5.refs_3_), channel_id=1, source_target_pairs={{0,8},{1,9},{2,10},{3,11},{4,12},{5,13},{6,14},{7,15},{8,0},{9,1},... | collective-permute-start | bytes 356360 | tf_op jit(solution)/shard_map/ppermute | solution.py:16
  37.3 5.0 %collective-permute-start.11 = (bf16[16,3712]{1,0:T(8,128)(2,1)S(1)}, bf16[16,3712]{1,0:T(8,128)(2,1)S(1)}, u32[]{:S(2)}, u32[]{:S(2)}) collective-permute-start(bf16[16,3712]{1,0:T(8,128)(2,1)S(1)} %collective-permute-done.6.refs_5_), channel_id=1, source_target_pairs={{0,2},{1,3},{2,0},{3,1},{4,6},{5,7},{6,4},{7,5},{8,10},{9,11},{10,... | collective-permute-start | bytes 356360 | tf_op jit(solution)/shard_map/ppermute | solution.py:16
  41.4 4.8 %collective-permute-start.12 = (bf16[16,3712]{1,0:T(8,128)(2,1)S(1)}, bf16[16,3712]{1,0:T(8,128)(2,1)S(1)}, u32[]{:S(2)}, u32[]{:S(2)}) collective-permute-start(bf16[16,3712]{1,0:T(8,128)(2,1)S(1)} %collective-permute-done.7.refs_7_), channel_id=1, source_target_pairs={{0,4},{1,5},{2,6},{3,7},{4,0},{5,1},{6,2},{7,3},{8,12},{9,13},{10,... | collective-permute-start | bytes 356360 | tf_op jit(solution)/shard_map/ppermute | solution.py:16
  42.4 9.1 %collective-permute-start.14 = (bf16[16,3712]{1,0:T(8,128)(2,1)S(1)}, bf16[16,3712]{1,0:T(8,128)(2,1)S(1)}, u32[]{:S(2)}, u32[]{:S(2)}) collective-permute-start(bf16[16,3712]{1,0:T(8,128)(2,1)S(1)} %collective-permute-done.9.refs_10_), channel_id=1, source_target_pairs={{0,2},{1,3},{2,0},{3,1},{4,6},{5,7},{6,4},{7,5},{8,10},{9,11},{10,... | collective-permute-start | bytes 356360 | tf_op jit(solution)/shard_map/ppermute | solution.py:16
  46.3 5.2 %collective-permute-start.15 = (bf16[16,3712]{1,0:T(8,128)(2,1)S(1)}, bf16[16,3712]{1,0:T(8,128)(2,1)S(1)}, u32[]{:S(2)}, u32[]{:S(2)}) collective-permute-start(bf16[16,3712]{1,0:T(8,128)(2,1)S(1)} %collective-permute-done.13.refs_13_), channel_id=1, source_target_pairs={{0,4},{1,5},{2,6},{3,7},{4,0},{5,1},{6,2},{7,3},{8,12},{9,13},{10,... | collective-permute-start | bytes 356360 | tf_op jit(solution)/shard_map/ppermute | solution.py:16
  59.8 4.9 %collective-permute-start.24 = (bf16[16,3584]{1,0:T(8,128)(2,1)S(1)}, bf16[16,3584]{1,0:T(8,128)(2,1)S(1)}, u32[]{:S(2)}, u32[]{:S(2)}) collective-permute-start(bf16[16,3584]{1,0:T(8,128)(2,1)S(1)} %get-tuple-element.58), channel_id=1, source_target_pairs={{0,2},{1,3},{2,0},{3,1},{4,6},{5,7},{6,4},{7,5},{8,10},{9,11},{10,... | collective-permute-start | bytes 344072 | tf_op jit(solution)/shard_map/ppermute | solution.py:16
  61.4 5.5 %collective-permute-start.19 = (bf16[16,3584]{1,0:T(8,128)(2,1)S(1)}, bf16[16,3584]{1,0:T(8,128)(2,1)S(1)}, u32[]{:S(2)}, u32[]{:S(2)}) collective-permute-start(bf16[16,3584]{1,0:T(8,128)(2,1)S(1)} %get-tuple-element.57), channel_id=1, source_target_pairs={{0,4},{1,5},{2,6},{3,7},{4,0},{5,1},{6,2},{7,3},{8,12},{9,13},{10,... | collective-permute-start | bytes 344072 | tf_op jit(solution)/shard_map/ppermute | solution.py:16
  62.6 7.2 %collective-permute-start.22 = (bf16[32,3584]{1,0:T(8,128)(2,1)S(1)}, bf16[32,3584]{1,0:T(8,128)(2,1)S(1)}, u32[]{:S(2)}, u32[]{:S(2)}) collective-permute-start(bf16[32,3584]{1,0:T(8,128)(2,1)S(1)} %get-tuple-element.48), channel_id=1, source_target_pairs={{0,2},{1,3},{2,0},{3,1},{4,6},{5,7},{6,4},{7,5},{8,10},{9,11},{10,... | collective-permute-start | bytes 688136 | tf_op jit(solution)/shard_map/ppermute | solution.py:16
  64.8 6.2 %collective-permute-start.25 = (bf16[32,3584]{1,0:T(8,128)(2,1)S(1)}, bf16[32,3584]{1,0:T(8,128)(2,1)S(1)}, u32[]{:S(2)}, u32[]{:S(2)}) collective-permute-start(bf16[32,3584]{1,0:T(8,128)(2,1)S(1)} %pad_maximum_fusion.1), channel_id=1, source_target_pairs={{0,4},{1,5},{2,6},{3,7},{4,0},{5,1},{6,2},{7,3},{8,12},{9,13},{10,... | collective-permute-start | bytes 688136 | tf_op jit(solution)/shard_map/ppermute | solution.py:16
  66.9 6.6 %collective-permute-start.20 = (bf16[32,3584]{1,0:T(8,128)(2,1)S(1)}, bf16[32,3584]{1,0:T(8,128)(2,1)S(1)}, u32[]{:S(2)}, u32[]{:S(2)}) collective-permute-start(bf16[32,3584]{1,0:T(8,128)(2,1)S(1)} %pad_maximum_fusion), channel_id=1, source_target_pairs={{0,8},{1,9},{2,10},{3,11},{4,12},{5,13},{6,14},{7,15},{8,0},{9,1},... | collective-permute-start | bytes 688136 | tf_op jit(solution)/shard_map/ppermute | solution.py:16
  69.9 6.2 %collective-permute-start.28 = (bf16[16,3584]{1,0:T(8,128)(2,1)S(1)}, bf16[16,3584]{1,0:T(8,128)(2,1)S(1)}, u32[]{:S(2)}, u32[]{:S(2)}) collective-permute-start(bf16[16,3584]{1,0:T(8,128)(2,1)S(1)} %get-tuple-element.54), channel_id=1, source_target_pairs={{0,4},{1,5},{2,6},{3,7},{4,0},{5,1},{6,2},{7,3},{8,12},{9,13},{10,... | collective-permute-start | bytes 344072 | tf_op jit(solution)/shard_map/ppermute | solution.py:16
  71.0 6.6 %collective-permute-start.29 = (bf16[16,3584]{1,0:T(8,128)(2,1)S(1)}, bf16[16,3584]{1,0:T(8,128)(2,1)S(1)}, u32[]{:S(2)}, u32[]{:S(2)}) collective-permute-start(bf16[16,3584]{1,0:T(8,128)(2,1)S(1)} %get-tuple-element.56), channel_id=1, source_target_pairs={{0,8},{1,9},{2,10},{3,11},{4,12},{5,13},{6,14},{7,15},{8,0},{9,1},... | collective-permute-start | bytes 344072 | tf_op jit(solution)/shard_map/ppermute | solution.py:16
  73.6 4.9 %collective-permute-start.27 = (bf16[16,3584]{1,0:T(8,128)(2,1)S(1)}, bf16[16,3584]{1,0:T(8,128)(2,1)S(1)}, u32[]{:S(2)}, u32[]{:S(2)}) collective-permute-start(bf16[16,3584]{1,0:T(8,128)(2,1)S(1)} %get-tuple-element.52), channel_id=1, source_target_pairs={{0,2},{1,3},{2,0},{3,1},{4,6},{5,7},{6,4},{7,5},{8,10},{9,11},{10,... | collective-permute-start | bytes 344072 | tf_op jit(solution)/shard_map/ppermute | solution.py:16
  75.3 4.8 %collective-permute-start.23 = (bf16[16,3584]{1,0:T(8,128)(2,1)S(1)}, bf16[16,3584]{1,0:T(8,128)(2,1)S(1)}, u32[]{:S(2)}, u32[]{:S(2)}) collective-permute-start(bf16[16,3584]{1,0:T(8,128)(2,1)S(1)} %get-tuple-element.53), channel_id=1, source_target_pairs={{0,4},{1,5},{2,6},{3,7},{4,0},{5,1},{6,2},{7,3},{8,12},{9,13},{10,... | collective-permute-start | bytes 344072 | tf_op jit(solution)/shard_map/ppermute | solution.py:16
  76.1 4.8 %collective-permute-start.26 = (bf16[16,3584]{1,0:T(8,128)(2,1)S(1)}, bf16[16,3584]{1,0:T(8,128)(2,1)S(1)}, u32[]{:S(2)}, u32[]{:S(2)}) collective-permute-start(bf16[16,3584]{1,0:T(8,128)(2,1)S(1)} %get-tuple-element.55), channel_id=1, source_target_pairs={{0,8},{1,9},{2,10},{3,11},{4,12},{5,13},{6,14},{7,15},{8,0},{9,1},... | collective-permute-start | bytes 344072 | tf_op jit(solution)/shard_map/ppermute | solution.py:16
  76.1 4.8 %collective-permute-start.21 = (bf16[16,3584]{1,0:T(8,128)(2,1)S(1)}, bf16[16,3584]{1,0:T(8,128)(2,1)S(1)}, u32[]{:S(2)}, u32[]{:S(2)}) collective-permute-start(bf16[16,3584]{1,0:T(8,128)(2,1)S(1)} %get-tuple-element.51), channel_id=1, source_target_pairs={{0,2},{1,3},{2,0},{3,1},{4,6},{5,7},{6,4},{7,5},{8,10},{9,11},{10,... | collective-permute-start | bytes 344072 | tf_op jit(solution)/shard_map/ppermute | solution.py:16
  78.5 7.0 %collective-permute-start.30 = (bf16[16,3584]{1,0:T(8,128)(2,1)S(1)}, bf16[16,3584]{1,0:T(8,128)(2,1)S(1)}, u32[]{:S(2)}, u32[]{:S(2)}) collective-permute-start(bf16[16,3584]{1,0:T(8,128)(2,1)S(1)} %add_convert_fusion.1), channel_id=1, source_target_pairs={{0,16},{1,17},{2,18},{3,19},{4,20},{5,21},{6,22},{7,23},{8,24},{9,... | collective-permute-start | bytes 344072 | tf_op jit(solution)/shard_map/ppermute | solution.py:16
where the time goes:
time: 86.4 us; the launch traced here: 86.2 us
  waiting for transfers between devices  40.7 us (47%)
  starting transfers between devices  29.1 us (34%)
  Pallas kernels  12.6 us (15%)
  other arithmetic  2.2 us (3%)
  local copies, waits for them, and re-layouts  1.56 us (2%)
    ppermute x31, waiting for transfers between devices, exchange(): return lax.ppermute(value, 'ep', pairs)  40.7 us
    ppermute x31, starting transfers between devices, exchange(): return lax.ppermute(value, 'ep', pairs)  29.1 us
    pallas_call x1, Pallas kernels, run_expert(): pl.pallas_call(functools.partial(expert_kernel, len(pieces), expert_count...  8.33 us
    pallas_call x1, Pallas kernels, load_weights(): pl.pallas_call(load_kernel, out_shape=[jax.ShapeDtypeStruct(value.shape,...  4.23 us
  transfers between devices with their start and end apart: 31, of which 19 were waited for; matrix products, arithmetic and copies ran while one was open for 4% of the time, Pallas kernels for 5%

commit v1 on v0

--- a/solution.py
+++ b/solution.py
@@ -38,11 +38,10 @@
     held = {0: own}
     for step in tree_plan(bits):
         for bit, masks in step:
-            arrived = exchange(joined([held[mask ^ (1 << bit)] for mask in masks]), 2 << bit)
+            sent = joined([held[mask ^ (1 << bit)] for mask in masks])
+            arrived = exchange(sent, 2 << bit)
             for place, mask in enumerate(masks):
                 held[mask] = arrived[count * place : count * (place + 1)]
-        masks = [mask for _, group in step for mask in group]
-        held.update(zip(masks, lax.optimization_barrier([held[mask] for mask in masks])))
     last = (1 << bits) - 1
     held[last] = exchange(held[last ^ (1 << last_bit)], 2 << last_bit)
     return held

time: 86.4 us -> 87.6 us (1.014)
  waiting for transfers between devices: 40.7 us -> 42.4 us
    ppermute x31, waiting for transfers between devices: 40.7 us -> 42.4 us  [exchange(): return lax.ppermute(value, 'ep', pairs)]
  transfers between devices with their start and end apart: 31 -> 31, of which waited for: 19 -> 21; matrix products, arithmetic and copies ran while one was open for 4% -> 3% of each run, Pallas kernels for 5% -> 5%
where the time goes in v1:
time: 87.6 us; the launch traced here: 87.4 us
  waiting for transfers between devices  42.4 us (48%)
  starting transfers between devices  28.5 us (33%)
  Pallas kernels  12.6 us (14%)
  other arithmetic  2.2 us (3%)
  local copies, waits for them, and re-layouts  1.57 us (2%)
    ppermute x31, waiting for transfers between devices, exchange(): return lax.ppermute(value, 'ep', pairs)  42.4 us
    ppermute x31, starting transfers between devices, exchange(): return lax.ppermute(value, 'ep', pairs)  28.5 us
    pallas_call x1, Pallas kernels, run_expert(): pl.pallas_call(functools.partial(expert_kernel, len(pieces), expert_count...  8.33 us
    pallas_call x1, Pallas kernels, load_weights(): pl.pallas_call(load_kernel, out_shape=[jax.ShapeDtypeStruct(value.shape,...  4.23 us
  transfers between devices with their start and end apart: 31, of which 21 were waited for; matrix products, arithmetic and copies ran while one was open for 3% of the time, Pallas kernels for 5%

profile of v1, /device:TPU:0, one launch (start us, length us, event | category | flops | bytes accessed | tf_op | source)
XLA Modules:
  0.0 87.4 jit_solution(6209770642620128500)
XLA Ops:
  2.7 3.6 %collective-permute-start.1 = (bf16[16,128]{1,0:T(8,128)(2,1)S(1)}, bf16[16,128]{1,0:T(8,128)(2,1)S(1)}, u32[]{:S(2)}, u32[]{:S(2)}) collective-permute-start(bf16[16,128]{1,0:T(8,128)(2,1)S(1)} %fusion.6), channel_id=1, source_target_pairs={{0,16},{1,17},{2,18},{3,19},{4,20},{5,21},{6,22},{7,23},{8,24},{9,... | collective-permute-start | bytes 12296 | tf_op jit(solution)/shard_map/ppermute | solution.py:16
  7.9 1.9 %collective-permute-start.6 = (bf16[16,3712]{1,0:T(8,128)(2,1)S(1)}, bf16[16,3712]{1,0:T(8,128)(2,1)S(1)}, u32[]{:S(2)}, u32[]{:S(2)}) collective-permute-start(bf16[16,3712]{1,0:T(8,128)(2,1)S(1)} %pad_maximum_fusion.2.refs_0_), channel_id=1, source_target_pairs={{0,8},{1,9},{2,10},{3,11},{4,12},{5,13},{6,14},{7,15},{8,0},{9,1},... | collective-permute-start | bytes 356360 | tf_op jit(solution)/shard_map/ppermute | solution.py:16
  9.8 5.4 %collective-permute-done = bf16[16,3584]{1,0:T(8,128)(2,1)S(1)} collective-permute-done((bf16[16,3584]{1,0:T(8,128)(2,1)}, bf16[16,3584]{1,0:T(8,128)(2,1)S(1)}, u32[]{:S(2)}, u32[]{:S(2)}) %collective-permute-start) | collective-permute-done | bytes 114720 | tf_op jit(solution)/shard_map/ppermute | solution.py:16
  15.2 1.5 %collective-permute-start.4 = (bf16[16,3712]{1,0:T(8,128)(2,1)S(1)}, bf16[16,3712]{1,0:T(8,128)(2,1)S(1)}, u32[]{:S(2)}, u32[]{:S(2)}) collective-permute-start(bf16[16,3712]{1,0:T(8,128)(2,1)S(1)} %pad_maximum_fusion.2.refs_0_), channel_id=1, source_target_pairs={{0,4},{1,5},{2,6},{3,7},{4,0},{5,1},{6,2},{7,3},{8,12},{9,13},{10,... | collective-permute-start | bytes 356360 | tf_op jit(solution)/shard_map/ppermute | solution.py:16
  16.8 1.6 %collective-permute-start.2 = (bf16[16,3712]{1,0:T(8,128)(2,1)S(1)}, bf16[16,3712]{1,0:T(8,128)(2,1)S(1)}, u32[]{:S(2)}, u32[]{:S(2)}) collective-permute-start(bf16[16,3712]{1,0:T(8,128)(2,1)S(1)} %pad_maximum_fusion.2.refs_0_), channel_id=1, source_target_pairs={{0,2},{1,3},{2,0},{3,1},{4,6},{5,7},{6,4},{7,5},{8,10},{9,11},{10,... | collective-permute-start | bytes 356360 | tf_op jit(solution)/shard_map/ppermute | solution.py:16
  18.3 1.7 %collective-permute-done.4.refs_4_ = bf16[16,3712]{1,0:T(8,128)(2,1)S(1)} collective-permute-done((bf16[16,3712]{1,0:T(8,128)(2,1)S(1)}, bf16[16,3712]{1,0:T(8,128)(2,1)S(1)}, u32[]{:S(2)}, u32[]{:S(2)}) %collective-permute-start.4) | collective-permute-done | bytes 118816 | tf_op jit(solution)/shard_map/ppermute | solution.py:16
  20.1 1.6 %collective-permute-done.2.refs_2_ = bf16[16,3712]{1,0:T(8,128)(2,1)S(1)} collective-permute-done((bf16[16,3712]{1,0:T(8,128)(2,1)S(1)}, bf16[16,3712]{1,0:T(8,128)(2,1)S(1)}, u32[]{:S(2)}, u32[]{:S(2)}) %collective-permute-start.2) | collective-permute-done | bytes 118816 | tf_op jit(solution)/shard_map/ppermute | solution.py:16
  22.2 2.7 %collective-permute-done.7.refs_7_ = bf16[16,3712]{1,0:T(8,128)(2,1)S(1)} collective-permute-done((bf16[16,3712]{1,0:T(8,128)(2,1)S(1)}, bf16[16,3712]{1,0:T(8,128)(2,1)S(1)}, u32[]{:S(2)}, u32[]{:S(2)}) %collective-permute-start.7) | collective-permute-done | bytes 118816 | tf_op jit(solution)/shard_map/ppermute | solution.py:16
  24.9 1.5 %collective-permute-start.3 = (bf16[16,3712]{1,0:T(8,128)(2,1)S(1)}, bf16[16,3712]{1,0:T(8,128)(2,1)S(1)}, u32[]{:S(2)}, u32[]{:S(2)}) collective-permute-start(bf16[16,3712]{1,0:T(8,128)(2,1)S(1)} %constant_dynamic-update-slice_fusion.refs_1_), channel_id=1, source_target_pairs={{0,2},{1,3},{2,0},{3,1},{4,6},{5,7},{6,4},{7,5},{8,10},{9,11},{10,... | collective-permute-start | bytes 356360 | tf_op jit(solution)/shard_map/ppermute | solution.py:16
  26.6 1.3 %collective-permute-start.10 = (bf16[16,3712]{1,0:T(8,128)(2,1)S(1)}, bf16[16,3712]{1,0:T(8,128)(2,1)S(1)}, u32[]{:S(2)}, u32[]{:S(2)}) collective-permute-start(bf16[16,3712]{1,0:T(8,128)(2,1)S(1)} %collective-permute-done.6.refs_6_), channel_id=1, source_target_pairs={{0,4},{1,5},{2,6},{3,7},{4,0},{5,1},{6,2},{7,3},{8,12},{9,13},{10,... | collective-permute-start | bytes 356360 | tf_op jit(solution)/shard_map/ppermute | solution.py:16
  27.9 3.1 %collective-permute-done.3.refs_3_ = bf16[16,3712]{1,0:T(8,128)(2,1)S(1)} collective-permute-done((bf16[16,3712]{1,0:T(8,128)(2,1)S(1)}, bf16[16,3712]{1,0:T(8,128)(2,1)S(1)}, u32[]{:S(2)}, u32[]{:S(2)}) %collective-permute-start.3) | collective-permute-done | bytes 118816 | tf_op jit(solution)/shard_map/ppermute | solution.py:16
  31.0 1.5 %collective-permute-start.8 = (bf16[16,3712]{1,0:T(8,128)(2,1)S(1)}, bf16[16,3712]{1,0:T(8,128)(2,1)S(1)}, u32[]{:S(2)}, u32[]{:S(2)}) collective-permute-start(bf16[16,3712]{1,0:T(8,128)(2,1)S(1)} %collective-permute-done.4.refs_4_), channel_id=1, source_target_pairs={{0,2},{1,3},{2,0},{3,1},{4,6},{5,7},{6,4},{7,5},{8,10},{9,11},{10,... | collective-permute-start | bytes 356360 | tf_op jit(solution)/shard_map/ppermute | solution.py:16
  32.5 4.5 %collective-permute-done.8.refs_8_ = bf16[16,3712]{1,0:T(8,128)(2,1)S(1)} collective-permute-done((bf16[16,3712]{1,0:T(8,128)(2,1)S(1)}, bf16[16,3712]{1,0:T(8,128)(2,1)S(1)}, u32[]{:S(2)}, u32[]{:S(2)}) %collective-permute-start.8) | collective-permute-done | bytes 118816 | tf_op jit(solution)/shard_map/ppermute | solution.py:16
  37.0 1.0 %collective-permute-start.11 = (bf16[16,3712]{1,0:T(8,128)(2,1)S(1)}, bf16[16,3712]{1,0:T(8,128)(2,1)S(1)}, u32[]{:S(2)}, u32[]{:S(2)}) collective-permute-start(bf16[16,3712]{1,0:T(8,128)(2,1)S(1)} %collective-permute-done.7.refs_7_), channel_id=1, source_target_pairs={{0,4},{1,5},{2,6},{3,7},{4,0},{5,1},{6,2},{7,3},{8,12},{9,13},{10,... | collective-permute-start | bytes 356360 | tf_op jit(solution)/shard_map/ppermute | solution.py:16
  38.0 1.5 %collective-permute-start.9 = (bf16[16,3712]{1,0:T(8,128)(2,1)S(1)}, bf16[16,3712]{1,0:T(8,128)(2,1)S(1)}, u32[]{:S(2)}, u32[]{:S(2)}) collective-permute-start(bf16[16,3712]{1,0:T(8,128)(2,1)S(1)} %collective-permute-done.5.refs_5_), channel_id=1, source_target_pairs={{0,2},{1,3},{2,0},{3,1},{4,6},{5,7},{6,4},{7,5},{8,10},{9,11},{10,... | collective-permute-start | bytes 356360 | tf_op jit(solution)/shard_map/ppermute | solution.py:16
  39.5 2.7 %collective-permute-done.11.refs_11_ = bf16[16,3712]{1,0:T(8,128)(2,1)S(1)} collective-permute-done((bf16[16,3712]{1,0:T(8,128)(2,1)S(1)}, bf16[16,3712]{1,0:T(8,128)(2,1)S(1)}, u32[]{:S(2)}, u32[]{:S(2)}) %collective-permute-start.11) | collective-permute-done | bytes 118816 | tf_op jit(solution)/shard_map/ppermute | solution.py:16
  42.9 1.5 %collective-permute-start.14 = (bf16[16,3712]{1,0:T(8,128)(2,1)S(1)}, bf16[16,3712]{1,0:T(8,128)(2,1)S(1)}, u32[]{:S(2)}, u32[]{:S(2)}) collective-permute-start(bf16[16,3712]{1,0:T(8,128)(2,1)S(1)} %collective-permute-done.10.refs_10_), channel_id=1, source_target_pairs={{0,2},{1,3},{2,0},{3,1},{4,6},{5,7},{6,4},{7,5},{8,10},{9,11},{10,... | collective-permute-start | bytes 356360 | tf_op jit(solution)/shard_map/ppermute | solution.py:16
  44.3 2.7 %collective-permute-done.13.refs_13_ = bf16[16,3712]{1,0:T(8,128)(2,1)S(1)} collective-permute-done((bf16[16,3712]{1,0:T(8,128)(2,1)S(1)}, bf16[16,3712]{1,0:T(8,128)(2,1)S(1)}, u32[]{:S(2)}, u32[]{:S(2)}) %collective-permute-start.13) | collective-permute-done | bytes 118816 | tf_op jit(solution)/shard_map/ppermute | solution.py:16
  48.0 4.2 %shard_map.64 = (bf16[3584,512]{1,0:T(8,128)(2,1)S(1)}, bf16[3584,512]{1,0:T(8,128)(2,1)S(1)}, bf16[512,3584]{1,0:T(8,128)(2,1)S(1)}) custom-call(bf16[3584,512]{1,0:T(8,128)(2,1)} %bitcast.4, bf16[3584,512]{1,0:T(8,128)(2,1)} %bitcast.6, bf16[512,3584]{1,0:T(8,128)(2,1)} %bitcast.8), custom_call_target="tpu_custom_call" | custom-call | bytes 11010048 | tf_op jit(solution)/shard_map/pallas_call | solution.py:135
  52.3 8.3 %shard_map.65 = (bf16[32,3584]{1,0:T(8,128)(2,1)S(1)}, bf16[32,3584]{1,0:T(8,128)(2,1)S(1)}, bf16[32,3584]{1,0:T(8,128)(2,1)S(1)}, bf16[32,3584]{1,0:T(8,128)(2,...) custom-call(bf16[16,3712]{1,0:T(8,128)(2,1)S(1)} %pad_maximum_fusion, ...), custom_call_target="tpu_custom_call" | custom-call | flops 5637144576 | bytes 25690112 | tf_op jit(solution)/shard_map/pallas_call | solution.py:212
  60.6 1.2 %collective-permute-start.24 = (bf16[16,3584]{1,0:T(8,128)(2,1)S(1)}, bf16[16,3584]{1,0:T(8,128)(2,1)S(1)}, u32[]{:S(2)}, u32[]{:S(2)}) collective-permute-start(bf16[16,3584]{1,0:T(8,128)(2,1)S(1)} %get-tuple-element.34), channel_id=1, source_target_pairs={{0,2},{1,3},{2,0},{3,1},{4,6},{5,7},{6,4},{7,5},{8,10},{9,11},{10,... | collective-permute-start | bytes 344072 | tf_op jit(solution)/shard_map/ppermute | solution.py:16
  61.9 1.0 %collective-permute-start.19 = (bf16[16,3584]{1,0:T(8,128)(2,1)S(1)}, bf16[16,3584]{1,0:T(8,128)(2,1)S(1)}, u32[]{:S(2)}, u32[]{:S(2)}) collective-permute-start(bf16[16,3584]{1,0:T(8,128)(2,1)S(1)} %get-tuple-element.33), channel_id=1, source_target_pairs={{0,4},{1,5},{2,6},{3,7},{4,0},{5,1},{6,2},{7,3},{8,12},{9,13},{10,... | collective-permute-start | bytes 344072 | tf_op jit(solution)/shard_map/ppermute | solution.py:16
  62.9 1.0 %collective-permute-start.22 = (bf16[32,3584]{1,0:T(8,128)(2,1)S(1)}, bf16[32,3584]{1,0:T(8,128)(2,1)S(1)}, u32[]{:S(2)}, u32[]{:S(2)}) collective-permute-start(bf16[32,3584]{1,0:T(8,128)(2,1)S(1)} %get-tuple-element.24), channel_id=1, source_target_pairs={{0,2},{1,3},{2,0},{3,1},{4,6},{5,7},{6,4},{7,5},{8,10},{9,11},{10,... | collective-permute-start | bytes 688136 | tf_op jit(solution)/shard_map/ppermute | solution.py:16
  63.9 1.7 %collective-permute-done.24 = bf16[16,3584]{1,0:T(8,128)(2,1)S(1)} collective-permute-done((bf16[16,3584]{1,0:T(8,128)(2,1)S(1)}, bf16[16,3584]{1,0:T(8,128)(2,1)S(1)}, u32[]{:S(2)}, u32[]{:S(2)}) %collective-permute-start.24) | collective-permute-done | bytes 114720 | tf_op jit(solution)/shard_map/ppermute | solution.py:16
  65.7 1.7 %collective-permute-start.25 = (bf16[32,3584]{1,0:T(8,128)(2,1)S(1)}, bf16[32,3584]{1,0:T(8,128)(2,1)S(1)}, u32[]{:S(2)}, u32[]{:S(2)}) collective-permute-start(bf16[32,3584]{1,0:T(8,128)(2,1)S(1)} %pad_maximum_fusion.1), channel_id=1, source_target_pairs={{0,4},{1,5},{2,6},{3,7},{4,0},{5,1},{6,2},{7,3},{8,12},{9,13},{10,... | collective-permute-start | bytes 688136 | tf_op jit(solution)/shard_map/ppermute | solution.py:16
  68.0 2.4 %collective-permute-done.22 = bf16[32,3584]{1,0:T(8,128)(2,1)S(1)} collective-permute-done((bf16[32,3584]{1,0:T(8,128)(2,1)S(1)}, bf16[32,3584]{1,0:T(8,128)(2,1)S(1)}, u32[]{:S(2)}, u32[]{:S(2)}) %collective-permute-start.22) | collective-permute-done | bytes 229408 | tf_op jit(solution)/shard_map/ppermute | solution.py:16
  70.5 1.1 %collective-permute-start.28 = (bf16[16,3584]{1,0:T(8,128)(2,1)S(1)}, bf16[16,3584]{1,0:T(8,128)(2,1)S(1)}, u32[]{:S(2)}, u32[]{:S(2)}) collective-permute-start(bf16[16,3584]{1,0:T(8,128)(2,1)S(1)} %get-tuple-element.30), channel_id=1, source_target_pairs={{0,4},{1,5},{2,6},{3,7},{4,0},{5,1},{6,2},{7,3},{8,12},{9,13},{10,... | collective-permute-start | bytes 344072 | tf_op jit(solution)/shard_map/ppermute | solution.py:16
  71.9 3.0 %collective-permute-done.20 = bf16[32,3584]{1,0:T(8,128)(2,1)S(1)} collective-permute-done((bf16[32,3584]{1,0:T(8,128)(2,1)S(1)}, bf16[32,3584]{1,0:T(8,128)(2,1)S(1)}, u32[]{:S(2)}, u32[]{:S(2)}) %collective-permute-start.20) | collective-permute-done | bytes 229408 | tf_op jit(solution)/shard_map/ppermute | solution.py:16
  75.6 1.3 %collective-permute-start.23 = (bf16[16,3584]{1,0:T(8,128)(2,1)S(1)}, bf16[16,3584]{1,0:T(8,128)(2,1)S(1)}, u32[]{:S(2)}, u32[]{:S(2)}) collective-permute-start(bf16[16,3584]{1,0:T(8,128)(2,1)S(1)} %get-tuple-element.29), channel_id=1, source_target_pairs={{0,4},{1,5},{2,6},{3,7},{4,0},{5,1},{6,2},{7,3},{8,12},{9,13},{10,... | collective-permute-start | bytes 344072 | tf_op jit(solution)/shard_map/ppermute | solution.py:16
  77.7 2.1 %collective-permute-done.27 = bf16[16,3584]{1,0:T(8,128)(2,1)S(1)} collective-permute-done((bf16[16,3584]{1,0:T(8,128)(2,1)S(1)}, bf16[16,3584]{1,0:T(8,128)(2,1)S(1)}, u32[]{:S(2)}, u32[]{:S(2)}) %collective-permute-start.27) | collective-permute-done | bytes 114720 | tf_op jit(solution)/shard_map/ppermute | solution.py:16
  80.4 1.3 %collective-permute-done.26 = bf16[16,3584]{1,0:T(8,128)(2,1)S(1)} collective-permute-done((bf16[16,3584]{1,0:T(8,128)(2,1)S(1)}, bf16[16,3584]{1,0:T(8,128)(2,1)S(1)}, u32[]{:S(2)}, u32[]{:S(2)}) %collective-permute-start.26) | collective-permute-done | bytes 114720 | tf_op jit(solution)/shard_map/ppermute | solution.py:16
  82.0 4.6 %collective-permute-done.30 = bf16[16,3584]{1,0:T(8,128)(2,1)S(1)} collective-permute-done((bf16[16,3584]{1,0:T(8,128)(2,1)S(1)}, bf16[16,3584]{1,0:T(8,128)(2,1)S(1)}, u32[]{:S(2)}, u32[]{:S(2)}) %collective-permute-start.30) | collective-permute-done | bytes 114720 | tf_op jit(solution)/shard_map/ppermute | solution.py:16
  (52 shorter events, 11.0 us)
Async XLA Ops:
  0.0 52.3 %collective-permute-start.16 = (bf16[3584,512]{1,0:T(8,128)(2,1)}, bf16[3584,512]{1,0:T(8,128)(2,1)}, u32[]{:S(2)}, u32[]{:S(2)}) collective-permute-start(bf16[3584,512]{1,0:T(8,128)(2,1)} %bitcast.3), channel_id=1, source_target_pairs={{0,1},{1,0},{2,3},{3,2},{4,5},{5,4},{6,7},{7,6},{8,9},{9,8},{10,11... | collective-permute-start | bytes 11010056 | tf_op jit(solution)/shard_map/ppermute | solution.py:16
  0.5 51.8 %collective-permute-start.17 = (bf16[3584,512]{1,0:T(8,128)(2,1)}, bf16[3584,512]{1,0:T(8,128)(2,1)}, u32[]{:S(2)}, u32[]{:S(2)}) collective-permute-start(bf16[3584,512]{1,0:T(8,128)(2,1)} %bitcast.5), channel_id=1, source_target_pairs={{0,1},{1,0},{2,3},{3,2},{4,5},{5,4},{6,7},{7,6},{8,9},{9,8},{10,11... | collective-permute-start | bytes 11010056 | tf_op jit(solution)/shard_map/ppermute | solution.py:16
  0.5 51.8 %collective-permute-start.18 = (bf16[512,3584]{1,0:T(8,128)(2,1)}, bf16[512,3584]{1,0:T(8,128)(2,1)}, u32[]{:S(2)}, u32[]{:S(2)}) collective-permute-start(bf16[512,3584]{1,0:T(8,128)(2,1)} %bitcast.7), channel_id=1, source_target_pairs={{0,1},{1,0},{2,3},{3,2},{4,5},{5,4},{6,7},{7,6},{8,9},{9,8},{10,11... | collective-permute-start | bytes 11010056 | tf_op jit(solution)/shard_map/ppermute | solution.py:16
  2.7 5.2 %collective-permute-start.1 = (bf16[16,128]{1,0:T(8,128)(2,1)S(1)}, bf16[16,128]{1,0:T(8,128)(2,1)S(1)}, u32[]{:S(2)}, u32[]{:S(2)}) collective-permute-start(bf16[16,128]{1,0:T(8,128)(2,1)S(1)} %fusion.6), channel_id=1, source_target_pairs={{0,16},{1,17},{2,18},{3,19},{4,20},{5,21},{6,22},{7,23},{8,24},{9,... | collective-permute-start | bytes 12296 | tf_op jit(solution)/shard_map/ppermute | solution.py:16
  6.3 8.9 %collective-permute-start = (bf16[16,3584]{1,0:T(8,128)(2,1)}, bf16[16,3584]{1,0:T(8,128)(2,1)S(1)}, u32[]{:S(2)}, u32[]{:S(2)}) collective-permute-start(bf16[16,3584]{1,0:T(8,128)(2,1)} %param.6), channel_id=1, source_target_pairs={{0,16},{1,17},{2,18},{3,19},{4,20},{5,21},{6,22},{7,23},{8,24},{9,... | collective-permute-start | bytes 344072 | tf_op jit(solution)/shard_map/ppermute | solution.py:16
  7.9 8.9 %collective-permute-start.6 = (bf16[16,3712]{1,0:T(8,128)(2,1)S(1)}, bf16[16,3712]{1,0:T(8,128)(2,1)S(1)}, u32[]{:S(2)}, u32[]{:S(2)}) collective-permute-start(bf16[16,3712]{1,0:T(8,128)(2,1)S(1)} %pad_maximum_fusion.2.refs_0_), channel_id=1, source_target_pairs={{0,8},{1,9},{2,10},{3,11},{4,12},{5,13},{6,14},{7,15},{8,0},{9,1},... | collective-permute-start | bytes 356360 | tf_op jit(solution)/shard_map/ppermute | solution.py:16
  15.2 4.8 %collective-permute-start.4 = (bf16[16,3712]{1,0:T(8,128)(2,1)S(1)}, bf16[16,3712]{1,0:T(8,128)(2,1)S(1)}, u32[]{:S(2)}, u32[]{:S(2)}) collective-permute-start(bf16[16,3712]{1,0:T(8,128)(2,1)S(1)} %pad_maximum_fusion.2.refs_0_), channel_id=1, source_target_pairs={{0,4},{1,5},{2,6},{3,7},{4,0},{5,1},{6,2},{7,3},{8,12},{9,13},{10,... | collective-permute-start | bytes 356360 | tf_op jit(solution)/shard_map/ppermute | solution.py:16
  16.8 4.9 %collective-permute-start.2 = (bf16[16,3712]{1,0:T(8,128)(2,1)S(1)}, bf16[16,3712]{1,0:T(8,128)(2,1)S(1)}, u32[]{:S(2)}, u32[]{:S(2)}) collective-permute-start(bf16[16,3712]{1,0:T(8,128)(2,1)S(1)} %pad_maximum_fusion.2.refs_0_), channel_id=1, source_target_pairs={{0,2},{1,3},{2,0},{3,1},{4,6},{5,7},{6,4},{7,5},{8,10},{9,11},{10,... | collective-permute-start | bytes 356360 | tf_op jit(solution)/shard_map/ppermute | solution.py:16
  20.1 4.8 %collective-permute-start.7 = (bf16[16,3712]{1,0:T(8,128)(2,1)S(1)}, bf16[16,3712]{1,0:T(8,128)(2,1)S(1)}, u32[]{:S(2)}, u32[]{:S(2)}) collective-permute-start(bf16[16,3712]{1,0:T(8,128)(2,1)S(1)} %constant_dynamic-update-slice_fusion.refs_1_), channel_id=1, source_target_pairs={{0,8},{1,9},{2,10},{3,11},{4,12},{5,13},{6,14},{7,15},{8,0},{9,1},... | collective-permute-start | bytes 356360 | tf_op jit(solution)/shard_map/ppermute | solution.py:16
  21.7 4.9 %collective-permute-start.5 = (bf16[16,3712]{1,0:T(8,128)(2,1)S(1)}, bf16[16,3712]{1,0:T(8,128)(2,1)S(1)}, u32[]{:S(2)}, u32[]{:S(2)}) collective-permute-start(bf16[16,3712]{1,0:T(8,128)(2,1)S(1)} %constant_dynamic-update-slice_fusion.refs_1_), channel_id=1, source_target_pairs={{0,4},{1,5},{2,6},{3,7},{4,0},{5,1},{6,2},{7,3},{8,12},{9,13},{10,... | collective-permute-start | bytes 356360 | tf_op jit(solution)/shard_map/ppermute | solution.py:16
  24.9 6.1 %collective-permute-start.3 = (bf16[16,3712]{1,0:T(8,128)(2,1)S(1)}, bf16[16,3712]{1,0:T(8,128)(2,1)S(1)}, u32[]{:S(2)}, u32[]{:S(2)}) collective-permute-start(bf16[16,3712]{1,0:T(8,128)(2,1)S(1)} %constant_dynamic-update-slice_fusion.refs_1_), channel_id=1, source_target_pairs={{0,2},{1,3},{2,0},{3,1},{4,6},{5,7},{6,4},{7,5},{8,10},{9,11},{10,... | collective-permute-start | bytes 356360 | tf_op jit(solution)/shard_map/ppermute | solution.py:16
  26.6 5.9 %collective-permute-start.10 = (bf16[16,3712]{1,0:T(8,128)(2,1)S(1)}, bf16[16,3712]{1,0:T(8,128)(2,1)S(1)}, u32[]{:S(2)}, u32[]{:S(2)}) collective-permute-start(bf16[16,3712]{1,0:T(8,128)(2,1)S(1)} %collective-permute-done.6.refs_6_), channel_id=1, source_target_pairs={{0,4},{1,5},{2,6},{3,7},{4,0},{5,1},{6,2},{7,3},{8,12},{9,13},{10,... | collective-permute-start | bytes 356360 | tf_op jit(solution)/shard_map/ppermute | solution.py:16
  31.0 6.0 %collective-permute-start.8 = (bf16[16,3712]{1,0:T(8,128)(2,1)S(1)}, bf16[16,3712]{1,0:T(8,128)(2,1)S(1)}, u32[]{:S(2)}, u32[]{:S(2)}) collective-permute-start(bf16[16,3712]{1,0:T(8,128)(2,1)S(1)} %collective-permute-done.4.refs_4_), channel_id=1, source_target_pairs={{0,2},{1,3},{2,0},{3,1},{4,6},{5,7},{6,4},{7,5},{8,10},{9,11},{10,... | collective-permute-start | bytes 356360 | tf_op jit(solution)/shard_map/ppermute | solution.py:16
  32.5 5.5 %collective-permute-start.12 = (bf16[16,3712]{1,0:T(8,128)(2,1)S(1)}, bf16[16,3712]{1,0:T(8,128)(2,1)S(1)}, u32[]{:S(2)}, u32[]{:S(2)}) collective-permute-start(bf16[16,3712]{1,0:T(8,128)(2,1)S(1)} %collective-permute-done.2.refs_2_), channel_id=1, source_target_pairs={{0,8},{1,9},{2,10},{3,11},{4,12},{5,13},{6,14},{7,15},{8,0},{9,1},... | collective-permute-start | bytes 356360 | tf_op jit(solution)/shard_map/ppermute | solution.py:16
  37.0 5.2 %collective-permute-start.11 = (bf16[16,3712]{1,0:T(8,128)(2,1)S(1)}, bf16[16,3712]{1,0:T(8,128)(2,1)S(1)}, u32[]{:S(2)}, u32[]{:S(2)}) collective-permute-start(bf16[16,3712]{1,0:T(8,128)(2,1)S(1)} %collective-permute-done.7.refs_7_), channel_id=1, source_target_pairs={{0,4},{1,5},{2,6},{3,7},{4,0},{5,1},{6,2},{7,3},{8,12},{9,13},{10,... | collective-permute-start | bytes 356360 | tf_op jit(solution)/shard_map/ppermute | solution.py:16
  38.0 4.8 %collective-permute-start.9 = (bf16[16,3712]{1,0:T(8,128)(2,1)S(1)}, bf16[16,3712]{1,0:T(8,128)(2,1)S(1)}, u32[]{:S(2)}, u32[]{:S(2)}) collective-permute-start(bf16[16,3712]{1,0:T(8,128)(2,1)S(1)} %collective-permute-done.5.refs_5_), channel_id=1, source_target_pairs={{0,2},{1,3},{2,0},{3,1},{4,6},{5,7},{6,4},{7,5},{8,10},{9,11},{10,... | collective-permute-start | bytes 356360 | tf_op jit(solution)/shard_map/ppermute | solution.py:16
  42.2 4.8 %collective-permute-start.13 = (bf16[16,3712]{1,0:T(8,128)(2,1)S(1)}, bf16[16,3712]{1,0:T(8,128)(2,1)S(1)}, u32[]{:S(2)}, u32[]{:S(2)}) collective-permute-start(bf16[16,3712]{1,0:T(8,128)(2,1)S(1)} %collective-permute-done.3.refs_3_), channel_id=1, source_target_pairs={{0,8},{1,9},{2,10},{3,11},{4,12},{5,13},{6,14},{7,15},{8,0},{9,1},... | collective-permute-start | bytes 356360 | tf_op jit(solution)/shard_map/ppermute | solution.py:16
  42.9 9.4 %collective-permute-start.14 = (bf16[16,3712]{1,0:T(8,128)(2,1)S(1)}, bf16[16,3712]{1,0:T(8,128)(2,1)S(1)}, u32[]{:S(2)}, u32[]{:S(2)}) collective-permute-start(bf16[16,3712]{1,0:T(8,128)(2,1)S(1)} %collective-permute-done.10.refs_10_), channel_id=1, source_target_pairs={{0,2},{1,3},{2,0},{3,1},{4,6},{5,7},{6,4},{7,5},{8,10},{9,11},{10,... | collective-permute-start | bytes 356360 | tf_op jit(solution)/shard_map/ppermute | solution.py:16
  47.0 5.2 %collective-permute-start.15 = (bf16[16,3712]{1,0:T(8,128)(2,1)S(1)}, bf16[16,3712]{1,0:T(8,128)(2,1)S(1)}, u32[]{:S(2)}, u32[]{:S(2)}) collective-permute-start(bf16[16,3712]{1,0:T(8,128)(2,1)S(1)} %collective-permute-done.13.refs_13_), channel_id=1, source_target_pairs={{0,4},{1,5},{2,6},{3,7},{4,0},{5,1},{6,2},{7,3},{8,12},{9,13},{10,... | collective-permute-start | bytes 356360 | tf_op jit(solution)/shard_map/ppermute | solution.py:16
  60.6 5.0 %collective-permute-start.24 = (bf16[16,3584]{1,0:T(8,128)(2,1)S(1)}, bf16[16,3584]{1,0:T(8,128)(2,1)S(1)}, u32[]{:S(2)}, u32[]{:S(2)}) collective-permute-start(bf16[16,3584]{1,0:T(8,128)(2,1)S(1)} %get-tuple-element.34), channel_id=1, source_target_pairs={{0,2},{1,3},{2,0},{3,1},{4,6},{5,7},{6,4},{7,5},{8,10},{9,11},{10,... | collective-permute-start | bytes 344072 | tf_op jit(solution)/shard_map/ppermute | solution.py:16
  61.9 6.0 %collective-permute-start.19 = (bf16[16,3584]{1,0:T(8,128)(2,1)S(1)}, bf16[16,3584]{1,0:T(8,128)(2,1)S(1)}, u32[]{:S(2)}, u32[]{:S(2)}) collective-permute-start(bf16[16,3584]{1,0:T(8,128)(2,1)S(1)} %get-tuple-element.33), channel_id=1, source_target_pairs={{0,4},{1,5},{2,6},{3,7},{4,0},{5,1},{6,2},{7,3},{8,12},{9,13},{10,... | collective-permute-start | bytes 344072 | tf_op jit(solution)/shard_map/ppermute | solution.py:16
  62.9 7.5 %collective-permute-start.22 = (bf16[32,3584]{1,0:T(8,128)(2,1)S(1)}, bf16[32,3584]{1,0:T(8,128)(2,1)S(1)}, u32[]{:S(2)}, u32[]{:S(2)}) collective-permute-start(bf16[32,3584]{1,0:T(8,128)(2,1)S(1)} %get-tuple-element.24), channel_id=1, source_target_pairs={{0,2},{1,3},{2,0},{3,1},{4,6},{5,7},{6,4},{7,5},{8,10},{9,11},{10,... | collective-permute-start | bytes 688136 | tf_op jit(solution)/shard_map/ppermute | solution.py:16
  65.7 6.1 %collective-permute-start.25 = (bf16[32,3584]{1,0:T(8,128)(2,1)S(1)}, bf16[32,3584]{1,0:T(8,128)(2,1)S(1)}, u32[]{:S(2)}, u32[]{:S(2)}) collective-permute-start(bf16[32,3584]{1,0:T(8,128)(2,1)S(1)} %pad_maximum_fusion.1), channel_id=1, source_target_pairs={{0,4},{1,5},{2,6},{3,7},{4,0},{5,1},{6,2},{7,3},{8,12},{9,13},{10,... | collective-permute-start | bytes 688136 | tf_op jit(solution)/shard_map/ppermute | solution.py:16
  67.9 6.9 %collective-permute-start.20 = (bf16[32,3584]{1,0:T(8,128)(2,1)S(1)}, bf16[32,3584]{1,0:T(8,128)(2,1)S(1)}, u32[]{:S(2)}, u32[]{:S(2)}) collective-permute-start(bf16[32,3584]{1,0:T(8,128)(2,1)S(1)} %pad_maximum_fusion), channel_id=1, source_target_pairs={{0,8},{1,9},{2,10},{3,11},{4,12},{5,13},{6,14},{7,15},{8,0},{9,1},... | collective-permute-start | bytes 688136 | tf_op jit(solution)/shard_map/ppermute | solution.py:16
  70.5 6.8 %collective-permute-start.28 = (bf16[16,3584]{1,0:T(8,128)(2,1)S(1)}, bf16[16,3584]{1,0:T(8,128)(2,1)S(1)}, u32[]{:S(2)}, u32[]{:S(2)}) collective-permute-start(bf16[16,3584]{1,0:T(8,128)(2,1)S(1)} %get-tuple-element.30), channel_id=1, source_target_pairs={{0,4},{1,5},{2,6},{3,7},{4,0},{5,1},{6,2},{7,3},{8,12},{9,13},{10,... | collective-permute-start | bytes 344072 | tf_op jit(solution)/shard_map/ppermute | solution.py:16
  71.8 5.9 %collective-permute-start.29 = (bf16[16,3584]{1,0:T(8,128)(2,1)S(1)}, bf16[16,3584]{1,0:T(8,128)(2,1)S(1)}, u32[]{:S(2)}, u32[]{:S(2)}) collective-permute-start(bf16[16,3584]{1,0:T(8,128)(2,1)S(1)} %get-tuple-element.32), channel_id=1, source_target_pairs={{0,8},{1,9},{2,10},{3,11},{4,12},{5,13},{6,14},{7,15},{8,0},{9,1},... | collective-permute-start | bytes 344072 | tf_op jit(solution)/shard_map/ppermute | solution.py:16
  74.9 4.9 %collective-permute-start.27 = (bf16[16,3584]{1,0:T(8,128)(2,1)S(1)}, bf16[16,3584]{1,0:T(8,128)(2,1)S(1)}, u32[]{:S(2)}, u32[]{:S(2)}) collective-permute-start(bf16[16,3584]{1,0:T(8,128)(2,1)S(1)} %get-tuple-element.28), channel_id=1, source_target_pairs={{0,2},{1,3},{2,0},{3,1},{4,6},{5,7},{6,4},{7,5},{8,10},{9,11},{10,... | collective-permute-start | bytes 344072 | tf_op jit(solution)/shard_map/ppermute | solution.py:16
  75.6 4.8 %collective-permute-start.23 = (bf16[16,3584]{1,0:T(8,128)(2,1)S(1)}, bf16[16,3584]{1,0:T(8,128)(2,1)S(1)}, u32[]{:S(2)}, u32[]{:S(2)}) collective-permute-start(bf16[16,3584]{1,0:T(8,128)(2,1)S(1)} %get-tuple-element.29), channel_id=1, source_target_pairs={{0,4},{1,5},{2,6},{3,7},{4,0},{5,1},{6,2},{7,3},{8,12},{9,13},{10,... | collective-permute-start | bytes 344072 | tf_op jit(solution)/shard_map/ppermute | solution.py:16
  76.9 4.8 %collective-permute-start.26 = (bf16[16,3584]{1,0:T(8,128)(2,1)S(1)}, bf16[16,3584]{1,0:T(8,128)(2,1)S(1)}, u32[]{:S(2)}, u32[]{:S(2)}) collective-permute-start(bf16[16,3584]{1,0:T(8,128)(2,1)S(1)} %get-tuple-element.31), channel_id=1, source_target_pairs={{0,8},{1,9},{2,10},{3,11},{4,12},{5,13},{6,14},{7,15},{8,0},{9,1},... | collective-permute-start | bytes 344072 | tf_op jit(solution)/shard_map/ppermute | solution.py:16
  77.2 4.8 %collective-permute-start.21 = (bf16[16,3584]{1,0:T(8,128)(2,1)S(1)}, bf16[16,3584]{1,0:T(8,128)(2,1)S(1)}, u32[]{:S(2)}, u32[]{:S(2)}) collective-permute-start(bf16[16,3584]{1,0:T(8,128)(2,1)S(1)} %get-tuple-element.27), channel_id=1, source_target_pairs={{0,2},{1,3},{2,0},{3,1},{4,6},{5,7},{6,4},{7,5},{8,10},{9,11},{10,... | collective-permute-start | bytes 344072 | tf_op jit(solution)/shard_map/ppermute | solution.py:16
  79.8 6.8 %collective-permute-start.30 = (bf16[16,3584]{1,0:T(8,128)(2,1)S(1)}, bf16[16,3584]{1,0:T(8,128)(2,1)S(1)}, u32[]{:S(2)}, u32[]{:S(2)}) collective-permute-start(bf16[16,3584]{1,0:T(8,128)(2,1)S(1)} %add_convert_fusion.1), channel_id=1, source_target_pairs={{0,16},{1,17},{2,18},{3,19},{4,20},{5,21},{6,22},{7,23},{8,24},{9,... | collective-permute-start | bytes 344072 | tf_op jit(solution)/shard_map/ppermute | solution.py:16

commit v2 on v1

--- a/solution.py
+++ b/solution.py
@@ -8,7 +8,7 @@
 from jax.sharding import PartitionSpec as P
 
 
-RESIDENT, VMEM_MIB = 3, 20
+RESIDENT, VMEM_MIB = 6, 14
 
 
 def exchange(value, mask):
@@ -106,14 +106,19 @@
 
 
 def gate_columns(routes, gate_weights, expert_count):
-    hits = routes[:, :, None] == jnp.arange(expert_count, dtype=jnp.int32)[None, None, :]
-    left = jnp.sum(jnp.where(hits, gate_weights[:, :, None], 0.0), axis=1)
+    count = routes.shape[0]
+    experts = jnp.arange(expert_count, dtype=jnp.int32)[None, :, None]
+    hits = routes.T[:, None, :] == experts
+    left = jnp.sum(jnp.where(hits, gate_weights.T[:, None, :], 0.0), axis=0)
     pieces = []
     for _ in range(3):
         piece = lax.reduce_precision(left, 8, 7)
         pieces.append(piece.astype(jnp.bfloat16))
         left = left - piece
-    columns = jnp.concatenate(pieces, axis=1)
+    columns = jnp.concatenate(
+        [piece[start : start + count] for start in range(0, expert_count, count) for piece in pieces],
+        axis=1,
+    )
     return jnp.pad(columns, ((0, 0), (0, -columns.shape[1] % 128)))
 
 
@@ -143,7 +148,7 @@
     )(*weights)
 
 
-def expert_kernel(pieces, expert_count, width, chunk, splits, resident, *refs):
+def expert_kernel(pieces, width, chunk, splits, resident, *refs):
     piece_refs, weight_refs = refs[:pieces], list(refs[pieces : pieces + 6])
     out_refs = refs[pieces + 6 : pieces + 6 + pieces // 2]
     rows, hidden, *loaded = refs[pieces + 6 + pieces // 2 :]
@@ -168,9 +173,12 @@
     for place, piece_ref in enumerate(piece_refs):
         rows[place * count : (place + 1) * count, :] = piece_ref[:, :width]
         columns = piece_ref[:, width:].astype(jnp.float32)
+        row = lax.broadcasted_iota(jnp.int32, columns.shape, 0)
         lane = lax.broadcasted_iota(jnp.int32, columns.shape, 1)
-        mine = (lax.rem(lane, expert_count) == expert) & (lane < 3 * expert_count)
-        scales.append(jnp.sum(jnp.where(mine, columns, 0.0), axis=1, keepdims=True))
+        here = row == lax.rem(expert, count)
+        line = jnp.sum(jnp.where(here, columns, 0.0), axis=0, keepdims=True)
+        mine = (lax.rem(lane, count) == row) & (lax.div(lane, 3 * count) == lax.div(expert, count))
+        scales.append(jnp.sum(jnp.where(mine, line, 0.0), axis=1, keepdims=True))
     for half in range(2):
         totals = []
         for kind in range(2):
@@ -193,7 +201,7 @@
             out_refs[place // 2][target, cols] = piece.astype(jnp.bfloat16)
 
 
-def run_expert(pieces, weights, expert_count):
+def run_expert(pieces, weights):
     count = pieces[0].shape[0]
     units, width = weights[2].shape
     vmem, hbm = pl.BlockSpec(memory_space=pltpu.VMEM), pl.BlockSpec(memory_space=pltpu.HBM)
@@ -210,7 +218,7 @@
         pltpu.with_memory_space_constraint(value, pltpu.HBM) for value in weights[resident:]
     )
     return pl.pallas_call(
-        functools.partial(expert_kernel, len(pieces), expert_count, width, chunk, splits, resident),
+        functools.partial(expert_kernel, len(pieces), width, chunk, splits, resident),
         out_shape=[jax.ShapeDtypeStruct((2 * count, width), jnp.bfloat16)] * (len(pieces) // 2),
         in_specs=[vmem] * (len(pieces) + resident) + [hbm] * (6 - resident),
         out_specs=[vmem] * (len(pieces) // 2),
@@ -235,7 +243,7 @@
     held = gather_rows(tokens, columns, bits)
     order = sorted(held, key=lambda mask: mask.bit_count())
     pieces = [piece for mask in order for piece in held[mask]]
-    sums = run_expert(pieces, tuple(own) + swapped, expert_count)
+    sums = run_expert(pieces, tuple(own) + swapped)
     return reduce_rows(dict(zip(order, sums)), bits)
 
 

time: 87.6 us -> 84.4 us (0.963)
  Pallas kernels: 12.6 us -> 10.3 us
  local copies, waits for them, and re-layouts: 1.57 us -> 0.05 us
    pallas_call x1, Pallas kernels: 8.33 us -> 6.03 us  [run_expert(): pl.pallas_call(functools.partial(expert_kernel, len(pieces), width, chunk...]
    unnamed x3 -> x1, local copies, waits for them, and re-layouts: 1.52 us -> 0.01 us
where the time goes in v2:
time: 84.4 us; the launch traced here: 84.2 us
  waiting for transfers between devices  42.4 us (50%)
  starting transfers between devices  28.5 us (34%)
  Pallas kernels  10.3 us (12%)
  other arithmetic  2.8 us (3%)
    ppermute x31, waiting for transfers between devices, exchange(): return lax.ppermute(value, 'ep', pairs)  42.4 us
    ppermute x31, starting transfers between devices, exchange(): return lax.ppermute(value, 'ep', pairs)  28.5 us
    pallas_call x1, Pallas kernels, run_expert(): pl.pallas_call(functools.partial(expert_kernel, len(pieces), width, chunk...  6.03 us
    pallas_call x1, Pallas kernels, load_weights(): pl.pallas_call(load_kernel, out_shape=[jax.ShapeDtypeStruct(value.shape,...  4.23 us
  transfers between devices with their start and end apart: 31, of which 21 were waited for; matrix products, arithmetic and copies ran while one was open for 3% of the time, Pallas kernels for 5%

profile of v2, /device:TPU:0, one launch (start us, length us, event | category | flops | bytes accessed | tf_op | source)
XLA Modules:
  0.0 84.2 jit_solution(16453647155874216558)
XLA Ops:
  1.8 3.6 %collective-permute-start.1 = (bf16[16,128]{1,0:T(8,128)(2,1)S(1)}, bf16[16,128]{1,0:T(8,128)(2,1)S(1)}, u32[]{:S(2)}, u32[]{:S(2)}) collective-permute-start(bf16[16,128]{1,0:T(8,128)(2,1)S(1)} %fusion.6), channel_id=1, source_target_pairs={{0,16},{1,17},{2,18},{3,19},{4,20},{5,21},{6,22},{7,23},{8,24},{9,... | collective-permute-start | bytes 12296 | tf_op jit(solution)/shard_map/ppermute | solution.py:16
  7.0 1.9 %collective-permute-start.6 = (bf16[16,3712]{1,0:T(8,128)(2,1)S(1)}, bf16[16,3712]{1,0:T(8,128)(2,1)S(1)}, u32[]{:S(2)}, u32[]{:S(2)}) collective-permute-start(bf16[16,3712]{1,0:T(8,128)(2,1)S(1)} %pad_maximum_fusion.2.refs_0_), channel_id=1, source_target_pairs={{0,8},{1,9},{2,10},{3,11},{4,12},{5,13},{6,14},{7,15},{8,0},{9,1},... | collective-permute-start | bytes 356360 | tf_op jit(solution)/shard_map/ppermute | solution.py:16
  8.9 5.4 %collective-permute-done = bf16[16,3584]{1,0:T(8,128)(2,1)S(1)} collective-permute-done((bf16[16,3584]{1,0:T(8,128)(2,1)}, bf16[16,3584]{1,0:T(8,128)(2,1)S(1)}, u32[]{:S(2)}, u32[]{:S(2)}) %collective-permute-start) | collective-permute-done | bytes 114720 | tf_op jit(solution)/shard_map/ppermute | solution.py:16
  14.3 1.5 %collective-permute-start.4 = (bf16[16,3712]{1,0:T(8,128)(2,1)S(1)}, bf16[16,3712]{1,0:T(8,128)(2,1)S(1)}, u32[]{:S(2)}, u32[]{:S(2)}) collective-permute-start(bf16[16,3712]{1,0:T(8,128)(2,1)S(1)} %pad_maximum_fusion.2.refs_0_), channel_id=1, source_target_pairs={{0,4},{1,5},{2,6},{3,7},{4,0},{5,1},{6,2},{7,3},{8,12},{9,13},{10,... | collective-permute-start | bytes 356360 | tf_op jit(solution)/shard_map/ppermute | solution.py:16
  15.9 1.6 %collective-permute-start.2 = (bf16[16,3712]{1,0:T(8,128)(2,1)S(1)}, bf16[16,3712]{1,0:T(8,128)(2,1)S(1)}, u32[]{:S(2)}, u32[]{:S(2)}) collective-permute-start(bf16[16,3712]{1,0:T(8,128)(2,1)S(1)} %pad_maximum_fusion.2.refs_0_), channel_id=1, source_target_pairs={{0,2},{1,3},{2,0},{3,1},{4,6},{5,7},{6,4},{7,5},{8,10},{9,11},{10,... | collective-permute-start | bytes 356360 | tf_op jit(solution)/shard_map/ppermute | solution.py:16
  17.4 1.7 %collective-permute-done.4.refs_4_ = bf16[16,3712]{1,0:T(8,128)(2,1)S(1)} collective-permute-done((bf16[16,3712]{1,0:T(8,128)(2,1)S(1)}, bf16[16,3712]{1,0:T(8,128)(2,1)S(1)}, u32[]{:S(2)}, u32[]{:S(2)}) %collective-permute-start.4) | collective-permute-done | bytes 118816 | tf_op jit(solution)/shard_map/ppermute | solution.py:16
  19.2 1.6 %collective-permute-done.2.refs_2_ = bf16[16,3712]{1,0:T(8,128)(2,1)S(1)} collective-permute-done((bf16[16,3712]{1,0:T(8,128)(2,1)S(1)}, bf16[16,3712]{1,0:T(8,128)(2,1)S(1)}, u32[]{:S(2)}, u32[]{:S(2)}) %collective-permute-start.2) | collective-permute-done | bytes 118816 | tf_op jit(solution)/shard_map/ppermute | solution.py:16
  21.3 2.7 %collective-permute-done.7.refs_7_ = bf16[16,3712]{1,0:T(8,128)(2,1)S(1)} collective-permute-done((bf16[16,3712]{1,0:T(8,128)(2,1)S(1)}, bf16[16,3712]{1,0:T(8,128)(2,1)S(1)}, u32[]{:S(2)}, u32[]{:S(2)}) %collective-permute-start.7) | collective-permute-done | bytes 118816 | tf_op jit(solution)/shard_map/ppermute | solution.py:16
  24.0 1.5 %collective-permute-start.3 = (bf16[16,3712]{1,0:T(8,128)(2,1)S(1)}, bf16[16,3712]{1,0:T(8,128)(2,1)S(1)}, u32[]{:S(2)}, u32[]{:S(2)}) collective-permute-start(bf16[16,3712]{1,0:T(8,128)(2,1)S(1)} %constant_dynamic-update-slice_fusion.refs_1_), channel_id=1, source_target_pairs={{0,2},{1,3},{2,0},{3,1},{4,6},{5,7},{6,4},{7,5},{8,10},{9,11},{10,... | collective-permute-start | bytes 356360 | tf_op jit(solution)/shard_map/ppermute | solution.py:16
  25.7 1.3 %collective-permute-start.10 = (bf16[16,3712]{1,0:T(8,128)(2,1)S(1)}, bf16[16,3712]{1,0:T(8,128)(2,1)S(1)}, u32[]{:S(2)}, u32[]{:S(2)}) collective-permute-start(bf16[16,3712]{1,0:T(8,128)(2,1)S(1)} %collective-permute-done.6.refs_6_), channel_id=1, source_target_pairs={{0,4},{1,5},{2,6},{3,7},{4,0},{5,1},{6,2},{7,3},{8,12},{9,13},{10,... | collective-permute-start | bytes 356360 | tf_op jit(solution)/shard_map/ppermute | solution.py:16
  27.0 3.1 %collective-permute-done.3.refs_3_ = bf16[16,3712]{1,0:T(8,128)(2,1)S(1)} collective-permute-done((bf16[16,3712]{1,0:T(8,128)(2,1)S(1)}, bf16[16,3712]{1,0:T(8,128)(2,1)S(1)}, u32[]{:S(2)}, u32[]{:S(2)}) %collective-permute-start.3) | collective-permute-done | bytes 118816 | tf_op jit(solution)/shard_map/ppermute | solution.py:16
  30.1 1.5 %collective-permute-start.8 = (bf16[16,3712]{1,0:T(8,128)(2,1)S(1)}, bf16[16,3712]{1,0:T(8,128)(2,1)S(1)}, u32[]{:S(2)}, u32[]{:S(2)}) collective-permute-start(bf16[16,3712]{1,0:T(8,128)(2,1)S(1)} %collective-permute-done.4.refs_4_), channel_id=1, source_target_pairs={{0,2},{1,3},{2,0},{3,1},{4,6},{5,7},{6,4},{7,5},{8,10},{9,11},{10,... | collective-permute-start | bytes 356360 | tf_op jit(solution)/shard_map/ppermute | solution.py:16
  31.6 4.5 %collective-permute-done.8.refs_8_ = bf16[16,3712]{1,0:T(8,128)(2,1)S(1)} collective-permute-done((bf16[16,3712]{1,0:T(8,128)(2,1)S(1)}, bf16[16,3712]{1,0:T(8,128)(2,1)S(1)}, u32[]{:S(2)}, u32[]{:S(2)}) %collective-permute-start.8) | collective-permute-done | bytes 118816 | tf_op jit(solution)/shard_map/ppermute | solution.py:16
  36.1 1.0 %collective-permute-start.11 = (bf16[16,3712]{1,0:T(8,128)(2,1)S(1)}, bf16[16,3712]{1,0:T(8,128)(2,1)S(1)}, u32[]{:S(2)}, u32[]{:S(2)}) collective-permute-start(bf16[16,3712]{1,0:T(8,128)(2,1)S(1)} %collective-permute-done.7.refs_7_), channel_id=1, source_target_pairs={{0,4},{1,5},{2,6},{3,7},{4,0},{5,1},{6,2},{7,3},{8,12},{9,13},{10,... | collective-permute-start | bytes 356360 | tf_op jit(solution)/shard_map/ppermute | solution.py:16
  37.1 1.5 %collective-permute-start.9 = (bf16[16,3712]{1,0:T(8,128)(2,1)S(1)}, bf16[16,3712]{1,0:T(8,128)(2,1)S(1)}, u32[]{:S(2)}, u32[]{:S(2)}) collective-permute-start(bf16[16,3712]{1,0:T(8,128)(2,1)S(1)} %collective-permute-done.5.refs_5_), channel_id=1, source_target_pairs={{0,2},{1,3},{2,0},{3,1},{4,6},{5,7},{6,4},{7,5},{8,10},{9,11},{10,... | collective-permute-start | bytes 356360 | tf_op jit(solution)/shard_map/ppermute | solution.py:16
  38.6 2.7 %collective-permute-done.11.refs_11_ = bf16[16,3712]{1,0:T(8,128)(2,1)S(1)} collective-permute-done((bf16[16,3712]{1,0:T(8,128)(2,1)S(1)}, bf16[16,3712]{1,0:T(8,128)(2,1)S(1)}, u32[]{:S(2)}, u32[]{:S(2)}) %collective-permute-start.11) | collective-permute-done | bytes 118816 | tf_op jit(solution)/shard_map/ppermute | solution.py:16
  41.9 1.5 %collective-permute-start.14 = (bf16[16,3712]{1,0:T(8,128)(2,1)S(1)}, bf16[16,3712]{1,0:T(8,128)(2,1)S(1)}, u32[]{:S(2)}, u32[]{:S(2)}) collective-permute-start(bf16[16,3712]{1,0:T(8,128)(2,1)S(1)} %collective-permute-done.10.refs_10_), channel_id=1, source_target_pairs={{0,2},{1,3},{2,0},{3,1},{4,6},{5,7},{6,4},{7,5},{8,10},{9,11},{10,... | collective-permute-start | bytes 356360 | tf_op jit(solution)/shard_map/ppermute | solution.py:16
  43.4 2.7 %collective-permute-done.13.refs_13_ = bf16[16,3712]{1,0:T(8,128)(2,1)S(1)} collective-permute-done((bf16[16,3712]{1,0:T(8,128)(2,1)S(1)}, bf16[16,3712]{1,0:T(8,128)(2,1)S(1)}, u32[]{:S(2)}, u32[]{:S(2)}) %collective-permute-start.13) | collective-permute-done | bytes 118816 | tf_op jit(solution)/shard_map/ppermute | solution.py:16
  47.1 4.2 %shard_map.64 = (bf16[3584,512]{1,0:T(8,128)(2,1)S(1)}, bf16[3584,512]{1,0:T(8,128)(2,1)S(1)}, bf16[512,3584]{1,0:T(8,128)(2,1)S(1)}) custom-call(bf16[3584,512]{1,0:T(8,128)(2,1)} %bitcast.6, bf16[3584,512]{1,0:T(8,128)(2,1)} %bitcast.8, bf16[512,3584]{1,0:T(8,128)(2,1)} %bitcast.10), custom_call_target="tpu_custom_call" | custom-call | bytes 11010048 | tf_op jit(solution)/shard_map/pallas_call | solution.py:140
  51.4 6.0 %shard_map.65 = (bf16[32,3584]{1,0:T(8,128)(2,1)S(1)}, bf16[32,3584]{1,0:T(8,128)(2,1)S(1)}, bf16[32,3584]{1,0:T(8,128)(2,1)S(1)}, bf16[32,3584]{1,0:T(8,128)(2,...) custom-call(bf16[16,3712]{1,0:T(8,128)(2,1)S(1)} %pad_maximum_fusion, ...), custom_call_target="tpu_custom_call" | custom-call | flops 5637144576 | bytes 25690112 | tf_op jit(solution)/shard_map/pallas_call | solution.py:220
  57.4 1.2 %collective-permute-start.24 = (bf16[16,3584]{1,0:T(8,128)(2,1)S(1)}, bf16[16,3584]{1,0:T(8,128)(2,1)S(1)}, u32[]{:S(2)}, u32[]{:S(2)}) collective-permute-start(bf16[16,3584]{1,0:T(8,128)(2,1)S(1)} %get-tuple-element.34), channel_id=1, source_target_pairs={{0,2},{1,3},{2,0},{3,1},{4,6},{5,7},{6,4},{7,5},{8,10},{9,11},{10,... | collective-permute-start | bytes 344072 | tf_op jit(solution)/shard_map/ppermute | solution.py:16
  58.7 1.0 %collective-permute-start.19 = (bf16[16,3584]{1,0:T(8,128)(2,1)S(1)}, bf16[16,3584]{1,0:T(8,128)(2,1)S(1)}, u32[]{:S(2)}, u32[]{:S(2)}) collective-permute-start(bf16[16,3584]{1,0:T(8,128)(2,1)S(1)} %get-tuple-element.33), channel_id=1, source_target_pairs={{0,4},{1,5},{2,6},{3,7},{4,0},{5,1},{6,2},{7,3},{8,12},{9,13},{10,... | collective-permute-start | bytes 344072 | tf_op jit(solution)/shard_map/ppermute | solution.py:16
  59.7 1.0 %collective-permute-start.22 = (bf16[32,3584]{1,0:T(8,128)(2,1)S(1)}, bf16[32,3584]{1,0:T(8,128)(2,1)S(1)}, u32[]{:S(2)}, u32[]{:S(2)}) collective-permute-start(bf16[32,3584]{1,0:T(8,128)(2,1)S(1)} %get-tuple-element.24), channel_id=1, source_target_pairs={{0,2},{1,3},{2,0},{3,1},{4,6},{5,7},{6,4},{7,5},{8,10},{9,11},{10,... | collective-permute-start | bytes 688136 | tf_op jit(solution)/shard_map/ppermute | solution.py:16
  60.7 1.7 %collective-permute-done.24 = bf16[16,3584]{1,0:T(8,128)(2,1)S(1)} collective-permute-done((bf16[16,3584]{1,0:T(8,128)(2,1)S(1)}, bf16[16,3584]{1,0:T(8,128)(2,1)S(1)}, u32[]{:S(2)}, u32[]{:S(2)}) %collective-permute-start.24) | collective-permute-done | bytes 114720 | tf_op jit(solution)/shard_map/ppermute | solution.py:16
  62.5 1.7 %collective-permute-start.25 = (bf16[32,3584]{1,0:T(8,128)(2,1)S(1)}, bf16[32,3584]{1,0:T(8,128)(2,1)S(1)}, u32[]{:S(2)}, u32[]{:S(2)}) collective-permute-start(bf16[32,3584]{1,0:T(8,128)(2,1)S(1)} %pad_maximum_fusion.1), channel_id=1, source_target_pairs={{0,4},{1,5},{2,6},{3,7},{4,0},{5,1},{6,2},{7,3},{8,12},{9,13},{10,... | collective-permute-start | bytes 688136 | tf_op jit(solution)/shard_map/ppermute | solution.py:16
  64.8 2.4 %collective-permute-done.22 = bf16[32,3584]{1,0:T(8,128)(2,1)S(1)} collective-permute-done((bf16[32,3584]{1,0:T(8,128)(2,1)S(1)}, bf16[32,3584]{1,0:T(8,128)(2,1)S(1)}, u32[]{:S(2)}, u32[]{:S(2)}) %collective-permute-start.22) | collective-permute-done | bytes 229408 | tf_op jit(solution)/shard_map/ppermute | solution.py:16
  67.3 1.1 %collective-permute-start.28 = (bf16[16,3584]{1,0:T(8,128)(2,1)S(1)}, bf16[16,3584]{1,0:T(8,128)(2,1)S(1)}, u32[]{:S(2)}, u32[]{:S(2)}) collective-permute-start(bf16[16,3584]{1,0:T(8,128)(2,1)S(1)} %get-tuple-element.30), channel_id=1, source_target_pairs={{0,4},{1,5},{2,6},{3,7},{4,0},{5,1},{6,2},{7,3},{8,12},{9,13},{10,... | collective-permute-start | bytes 344072 | tf_op jit(solution)/shard_map/ppermute | solution.py:16
  68.7 2.9 %collective-permute-done.20 = bf16[32,3584]{1,0:T(8,128)(2,1)S(1)} collective-permute-done((bf16[32,3584]{1,0:T(8,128)(2,1)S(1)}, bf16[32,3584]{1,0:T(8,128)(2,1)S(1)}, u32[]{:S(2)}, u32[]{:S(2)}) %collective-permute-start.20) | collective-permute-done | bytes 229408 | tf_op jit(solution)/shard_map/ppermute | solution.py:16
  72.4 1.3 %collective-permute-start.23 = (bf16[16,3584]{1,0:T(8,128)(2,1)S(1)}, bf16[16,3584]{1,0:T(8,128)(2,1)S(1)}, u32[]{:S(2)}, u32[]{:S(2)}) collective-permute-start(bf16[16,3584]{1,0:T(8,128)(2,1)S(1)} %get-tuple-element.29), channel_id=1, source_target_pairs={{0,4},{1,5},{2,6},{3,7},{4,0},{5,1},{6,2},{7,3},{8,12},{9,13},{10,... | collective-permute-start | bytes 344072 | tf_op jit(solution)/shard_map/ppermute | solution.py:16
  74.5 2.1 %collective-permute-done.27 = bf16[16,3584]{1,0:T(8,128)(2,1)S(1)} collective-permute-done((bf16[16,3584]{1,0:T(8,128)(2,1)S(1)}, bf16[16,3584]{1,0:T(8,128)(2,1)S(1)}, u32[]{:S(2)}, u32[]{:S(2)}) %collective-permute-start.27) | collective-permute-done | bytes 114720 | tf_op jit(solution)/shard_map/ppermute | solution.py:16
  77.2 1.3 %collective-permute-done.26 = bf16[16,3584]{1,0:T(8,128)(2,1)S(1)} collective-permute-done((bf16[16,3584]{1,0:T(8,128)(2,1)S(1)}, bf16[16,3584]{1,0:T(8,128)(2,1)S(1)}, u32[]{:S(2)}, u32[]{:S(2)}) %collective-permute-start.26) | collective-permute-done | bytes 114720 | tf_op jit(solution)/shard_map/ppermute | solution.py:16
  78.8 4.6 %collective-permute-done.30 = bf16[16,3584]{1,0:T(8,128)(2,1)S(1)} collective-permute-done((bf16[16,3584]{1,0:T(8,128)(2,1)S(1)}, bf16[16,3584]{1,0:T(8,128)(2,1)S(1)}, u32[]{:S(2)}, u32[]{:S(2)}) %collective-permute-start.30) | collective-permute-done | bytes 114720 | tf_op jit(solution)/shard_map/ppermute | solution.py:16
  (50 shorter events, 10.1 us)
Async XLA Ops:
  0.0 51.3 %collective-permute-start.16 = (bf16[3584,512]{1,0:T(8,128)(2,1)}, bf16[3584,512]{1,0:T(8,128)(2,1)S(1)}, u32[]{:S(2)}, u32[]{:S(2)}) collective-permute-start(bf16[3584,512]{1,0:T(8,128)(2,1)} %bitcast.5), channel_id=1, source_target_pairs={{0,1},{1,0},{2,3},{3,2},{4,5},{5,4},{6,7},{7,6},{8,9},{9,8},{10,11... | collective-permute-start | bytes 11010056 | tf_op jit(solution)/shard_map/ppermute | solution.py:16
  0.5 50.9 %collective-permute-start.17 = (bf16[3584,512]{1,0:T(8,128)(2,1)}, bf16[3584,512]{1,0:T(8,128)(2,1)S(1)}, u32[]{:S(2)}, u32[]{:S(2)}) collective-permute-start(bf16[3584,512]{1,0:T(8,128)(2,1)} %bitcast.7), channel_id=1, source_target_pairs={{0,1},{1,0},{2,3},{3,2},{4,5},{5,4},{6,7},{7,6},{8,9},{9,8},{10,11... | collective-permute-start | bytes 11010056 | tf_op jit(solution)/shard_map/ppermute | solution.py:16
  0.5 50.9 %collective-permute-start.18 = (bf16[512,3584]{1,0:T(8,128)(2,1)}, bf16[512,3584]{1,0:T(8,128)(2,1)S(1)}, u32[]{:S(2)}, u32[]{:S(2)}) collective-permute-start(bf16[512,3584]{1,0:T(8,128)(2,1)} %bitcast.9), channel_id=1, source_target_pairs={{0,1},{1,0},{2,3},{3,2},{4,5},{5,4},{6,7},{7,6},{8,9},{9,8},{10,11... | collective-permute-start | bytes 11010056 | tf_op jit(solution)/shard_map/ppermute | solution.py:16
  1.8 5.2 %collective-permute-start.1 = (bf16[16,128]{1,0:T(8,128)(2,1)S(1)}, bf16[16,128]{1,0:T(8,128)(2,1)S(1)}, u32[]{:S(2)}, u32[]{:S(2)}) collective-permute-start(bf16[16,128]{1,0:T(8,128)(2,1)S(1)} %fusion.6), channel_id=1, source_target_pairs={{0,16},{1,17},{2,18},{3,19},{4,20},{5,21},{6,22},{7,23},{8,24},{9,... | collective-permute-start | bytes 12296 | tf_op jit(solution)/shard_map/ppermute | solution.py:16
  5.4 8.9 %collective-permute-start = (bf16[16,3584]{1,0:T(8,128)(2,1)}, bf16[16,3584]{1,0:T(8,128)(2,1)S(1)}, u32[]{:S(2)}, u32[]{:S(2)}) collective-permute-start(bf16[16,3584]{1,0:T(8,128)(2,1)} %param.6), channel_id=1, source_target_pairs={{0,16},{1,17},{2,18},{3,19},{4,20},{5,21},{6,22},{7,23},{8,24},{9,... | collective-permute-start | bytes 344072 | tf_op jit(solution)/shard_map/ppermute | solution.py:16
  7.0 8.9 %collective-permute-start.6 = (bf16[16,3712]{1,0:T(8,128)(2,1)S(1)}, bf16[16,3712]{1,0:T(8,128)(2,1)S(1)}, u32[]{:S(2)}, u32[]{:S(2)}) collective-permute-start(bf16[16,3712]{1,0:T(8,128)(2,1)S(1)} %pad_maximum_fusion.2.refs_0_), channel_id=1, source_target_pairs={{0,8},{1,9},{2,10},{3,11},{4,12},{5,13},{6,14},{7,15},{8,0},{9,1},... | collective-permute-start | bytes 356360 | tf_op jit(solution)/shard_map/ppermute | solution.py:16
  14.3 4.8 %collective-permute-start.4 = (bf16[16,3712]{1,0:T(8,128)(2,1)S(1)}, bf16[16,3712]{1,0:T(8,128)(2,1)S(1)}, u32[]{:S(2)}, u32[]{:S(2)}) collective-permute-start(bf16[16,3712]{1,0:T(8,128)(2,1)S(1)} %pad_maximum_fusion.2.refs_0_), channel_id=1, source_target_pairs={{0,4},{1,5},{2,6},{3,7},{4,0},{5,1},{6,2},{7,3},{8,12},{9,13},{10,... | collective-permute-start | bytes 356360 | tf_op jit(solution)/shard_map/ppermute | solution.py:16
  15.9 4.9 %collective-permute-start.2 = (bf16[16,3712]{1,0:T(8,128)(2,1)S(1)}, bf16[16,3712]{1,0:T(8,128)(2,1)S(1)}, u32[]{:S(2)}, u32[]{:S(2)}) collective-permute-start(bf16[16,3712]{1,0:T(8,128)(2,1)S(1)} %pad_maximum_fusion.2.refs_0_), channel_id=1, source_target_pairs={{0,2},{1,3},{2,0},{3,1},{4,6},{5,7},{6,4},{7,5},{8,10},{9,11},{10,... | collective-permute-start | bytes 356360 | tf_op jit(solution)/shard_map/ppermute | solution.py:16
  19.2 4.8 %collective-permute-start.7 = (bf16[16,3712]{1,0:T(8,128)(2,1)S(1)}, bf16[16,3712]{1,0:T(8,128)(2,1)S(1)}, u32[]{:S(2)}, u32[]{:S(2)}) collective-permute-start(bf16[16,3712]{1,0:T(8,128)(2,1)S(1)} %constant_dynamic-update-slice_fusion.refs_1_), channel_id=1, source_target_pairs={{0,8},{1,9},{2,10},{3,11},{4,12},{5,13},{6,14},{7,15},{8,0},{9,1},... | collective-permute-start | bytes 356360 | tf_op jit(solution)/shard_map/ppermute | solution.py:16
  20.8 4.9 %collective-permute-start.5 = (bf16[16,3712]{1,0:T(8,128)(2,1)S(1)}, bf16[16,3712]{1,0:T(8,128)(2,1)S(1)}, u32[]{:S(2)}, u32[]{:S(2)}) collective-permute-start(bf16[16,3712]{1,0:T(8,128)(2,1)S(1)} %constant_dynamic-update-slice_fusion.refs_1_), channel_id=1, source_target_pairs={{0,4},{1,5},{2,6},{3,7},{4,0},{5,1},{6,2},{7,3},{8,12},{9,13},{10,... | collective-permute-start | bytes 356360 | tf_op jit(solution)/shard_map/ppermute | solution.py:16
  24.0 6.1 %collective-permute-start.3 = (bf16[16,3712]{1,0:T(8,128)(2,1)S(1)}, bf16[16,3712]{1,0:T(8,128)(2,1)S(1)}, u32[]{:S(2)}, u32[]{:S(2)}) collective-permute-start(bf16[16,3712]{1,0:T(8,128)(2,1)S(1)} %constant_dynamic-update-slice_fusion.refs_1_), channel_id=1, source_target_pairs={{0,2},{1,3},{2,0},{3,1},{4,6},{5,7},{6,4},{7,5},{8,10},{9,11},{10,... | collective-permute-start | bytes 356360 | tf_op jit(solution)/shard_map/ppermute | solution.py:16
  25.7 5.9 %collective-permute-start.10 = (bf16[16,3712]{1,0:T(8,128)(2,1)S(1)}, bf16[16,3712]{1,0:T(8,128)(2,1)S(1)}, u32[]{:S(2)}, u32[]{:S(2)}) collective-permute-start(bf16[16,3712]{1,0:T(8,128)(2,1)S(1)} %collective-permute-done.6.refs_6_), channel_id=1, source_target_pairs={{0,4},{1,5},{2,6},{3,7},{4,0},{5,1},{6,2},{7,3},{8,12},{9,13},{10,... | collective-permute-start | bytes 356360 | tf_op jit(solution)/shard_map/ppermute | solution.py:16
  30.1 6.0 %collective-permute-start.8 = (bf16[16,3712]{1,0:T(8,128)(2,1)S(1)}, bf16[16,3712]{1,0:T(8,128)(2,1)S(1)}, u32[]{:S(2)}, u32[]{:S(2)}) collective-permute-start(bf16[16,3712]{1,0:T(8,128)(2,1)S(1)} %collective-permute-done.4.refs_4_), channel_id=1, source_target_pairs={{0,2},{1,3},{2,0},{3,1},{4,6},{5,7},{6,4},{7,5},{8,10},{9,11},{10,... | collective-permute-start | bytes 356360 | tf_op jit(solution)/shard_map/ppermute | solution.py:16
  31.6 5.5 %collective-permute-start.12 = (bf16[16,3712]{1,0:T(8,128)(2,1)S(1)}, bf16[16,3712]{1,0:T(8,128)(2,1)S(1)}, u32[]{:S(2)}, u32[]{:S(2)}) collective-permute-start(bf16[16,3712]{1,0:T(8,128)(2,1)S(1)} %collective-permute-done.2.refs_2_), channel_id=1, source_target_pairs={{0,8},{1,9},{2,10},{3,11},{4,12},{5,13},{6,14},{7,15},{8,0},{9,1},... | collective-permute-start | bytes 356360 | tf_op jit(solution)/shard_map/ppermute | solution.py:16
  36.1 5.2 %collective-permute-start.11 = (bf16[16,3712]{1,0:T(8,128)(2,1)S(1)}, bf16[16,3712]{1,0:T(8,128)(2,1)S(1)}, u32[]{:S(2)}, u32[]{:S(2)}) collective-permute-start(bf16[16,3712]{1,0:T(8,128)(2,1)S(1)} %collective-permute-done.7.refs_7_), channel_id=1, source_target_pairs={{0,4},{1,5},{2,6},{3,7},{4,0},{5,1},{6,2},{7,3},{8,12},{9,13},{10,... | collective-permute-start | bytes 356360 | tf_op jit(solution)/shard_map/ppermute | solution.py:16
  37.1 4.8 %collective-permute-start.9 = (bf16[16,3712]{1,0:T(8,128)(2,1)S(1)}, bf16[16,3712]{1,0:T(8,128)(2,1)S(1)}, u32[]{:S(2)}, u32[]{:S(2)}) collective-permute-start(bf16[16,3712]{1,0:T(8,128)(2,1)S(1)} %collective-permute-done.5.refs_5_), channel_id=1, source_target_pairs={{0,2},{1,3},{2,0},{3,1},{4,6},{5,7},{6,4},{7,5},{8,10},{9,11},{10,... | collective-permute-start | bytes 356360 | tf_op jit(solution)/shard_map/ppermute | solution.py:16
  41.3 4.8 %collective-permute-start.13 = (bf16[16,3712]{1,0:T(8,128)(2,1)S(1)}, bf16[16,3712]{1,0:T(8,128)(2,1)S(1)}, u32[]{:S(2)}, u32[]{:S(2)}) collective-permute-start(bf16[16,3712]{1,0:T(8,128)(2,1)S(1)} %collective-permute-done.3.refs_3_), channel_id=1, source_target_pairs={{0,8},{1,9},{2,10},{3,11},{4,12},{5,13},{6,14},{7,15},{8,0},{9,1},... | collective-permute-start | bytes 356360 | tf_op jit(solution)/shard_map/ppermute | solution.py:16
  41.9 9.4 %collective-permute-start.14 = (bf16[16,3712]{1,0:T(8,128)(2,1)S(1)}, bf16[16,3712]{1,0:T(8,128)(2,1)S(1)}, u32[]{:S(2)}, u32[]{:S(2)}) collective-permute-start(bf16[16,3712]{1,0:T(8,128)(2,1)S(1)} %collective-permute-done.10.refs_10_), channel_id=1, source_target_pairs={{0,2},{1,3},{2,0},{3,1},{4,6},{5,7},{6,4},{7,5},{8,10},{9,11},{10,... | collective-permute-start | bytes 356360 | tf_op jit(solution)/shard_map/ppermute | solution.py:16
  46.1 5.2 %collective-permute-start.15 = (bf16[16,3712]{1,0:T(8,128)(2,1)S(1)}, bf16[16,3712]{1,0:T(8,128)(2,1)S(1)}, u32[]{:S(2)}, u32[]{:S(2)}) collective-permute-start(bf16[16,3712]{1,0:T(8,128)(2,1)S(1)} %collective-permute-done.13.refs_13_), channel_id=1, source_target_pairs={{0,4},{1,5},{2,6},{3,7},{4,0},{5,1},{6,2},{7,3},{8,12},{9,13},{10,... | collective-permute-start | bytes 356360 | tf_op jit(solution)/shard_map/ppermute | solution.py:16
  57.4 5.0 %collective-permute-start.24 = (bf16[16,3584]{1,0:T(8,128)(2,1)S(1)}, bf16[16,3584]{1,0:T(8,128)(2,1)S(1)}, u32[]{:S(2)}, u32[]{:S(2)}) collective-permute-start(bf16[16,3584]{1,0:T(8,128)(2,1)S(1)} %get-tuple-element.34), channel_id=1, source_target_pairs={{0,2},{1,3},{2,0},{3,1},{4,6},{5,7},{6,4},{7,5},{8,10},{9,11},{10,... | collective-permute-start | bytes 344072 | tf_op jit(solution)/shard_map/ppermute | solution.py:16
  58.7 6.0 %collective-permute-start.19 = (bf16[16,3584]{1,0:T(8,128)(2,1)S(1)}, bf16[16,3584]{1,0:T(8,128)(2,1)S(1)}, u32[]{:S(2)}, u32[]{:S(2)}) collective-permute-start(bf16[16,3584]{1,0:T(8,128)(2,1)S(1)} %get-tuple-element.33), channel_id=1, source_target_pairs={{0,4},{1,5},{2,6},{3,7},{4,0},{5,1},{6,2},{7,3},{8,12},{9,13},{10,... | collective-permute-start | bytes 344072 | tf_op jit(solution)/shard_map/ppermute | solution.py:16
  59.7 7.5 %collective-permute-start.22 = (bf16[32,3584]{1,0:T(8,128)(2,1)S(1)}, bf16[32,3584]{1,0:T(8,128)(2,1)S(1)}, u32[]{:S(2)}, u32[]{:S(2)}) collective-permute-start(bf16[32,3584]{1,0:T(8,128)(2,1)S(1)} %get-tuple-element.24), channel_id=1, source_target_pairs={{0,2},{1,3},{2,0},{3,1},{4,6},{5,7},{6,4},{7,5},{8,10},{9,11},{10,... | collective-permute-start | bytes 688136 | tf_op jit(solution)/shard_map/ppermute | solution.py:16
  62.5 6.1 %collective-permute-start.25 = (bf16[32,3584]{1,0:T(8,128)(2,1)S(1)}, bf16[32,3584]{1,0:T(8,128)(2,1)S(1)}, u32[]{:S(2)}, u32[]{:S(2)}) collective-permute-start(bf16[32,3584]{1,0:T(8,128)(2,1)S(1)} %pad_maximum_fusion.1), channel_id=1, source_target_pairs={{0,4},{1,5},{2,6},{3,7},{4,0},{5,1},{6,2},{7,3},{8,12},{9,13},{10,... | collective-permute-start | bytes 688136 | tf_op jit(solution)/shard_map/ppermute | solution.py:16
  64.7 6.9 %collective-permute-start.20 = (bf16[32,3584]{1,0:T(8,128)(2,1)S(1)}, bf16[32,3584]{1,0:T(8,128)(2,1)S(1)}, u32[]{:S(2)}, u32[]{:S(2)}) collective-permute-start(bf16[32,3584]{1,0:T(8,128)(2,1)S(1)} %pad_maximum_fusion), channel_id=1, source_target_pairs={{0,8},{1,9},{2,10},{3,11},{4,12},{5,13},{6,14},{7,15},{8,0},{9,1},... | collective-permute-start | bytes 688136 | tf_op jit(solution)/shard_map/ppermute | solution.py:16
  67.3 6.8 %collective-permute-start.28 = (bf16[16,3584]{1,0:T(8,128)(2,1)S(1)}, bf16[16,3584]{1,0:T(8,128)(2,1)S(1)}, u32[]{:S(2)}, u32[]{:S(2)}) collective-permute-start(bf16[16,3584]{1,0:T(8,128)(2,1)S(1)} %get-tuple-element.30), channel_id=1, source_target_pairs={{0,4},{1,5},{2,6},{3,7},{4,0},{5,1},{6,2},{7,3},{8,12},{9,13},{10,... | collective-permute-start | bytes 344072 | tf_op jit(solution)/shard_map/ppermute | solution.py:16
  68.6 5.9 %collective-permute-start.29 = (bf16[16,3584]{1,0:T(8,128)(2,1)S(1)}, bf16[16,3584]{1,0:T(8,128)(2,1)S(1)}, u32[]{:S(2)}, u32[]{:S(2)}) collective-permute-start(bf16[16,3584]{1,0:T(8,128)(2,1)S(1)} %get-tuple-element.32), channel_id=1, source_target_pairs={{0,8},{1,9},{2,10},{3,11},{4,12},{5,13},{6,14},{7,15},{8,0},{9,1},... | collective-permute-start | bytes 344072 | tf_op jit(solution)/shard_map/ppermute | solution.py:16
  71.7 4.9 %collective-permute-start.27 = (bf16[16,3584]{1,0:T(8,128)(2,1)S(1)}, bf16[16,3584]{1,0:T(8,128)(2,1)S(1)}, u32[]{:S(2)}, u32[]{:S(2)}) collective-permute-start(bf16[16,3584]{1,0:T(8,128)(2,1)S(1)} %get-tuple-element.28), channel_id=1, source_target_pairs={{0,2},{1,3},{2,0},{3,1},{4,6},{5,7},{6,4},{7,5},{8,10},{9,11},{10,... | collective-permute-start | bytes 344072 | tf_op jit(solution)/shard_map/ppermute | solution.py:16
  72.4 4.8 %collective-permute-start.23 = (bf16[16,3584]{1,0:T(8,128)(2,1)S(1)}, bf16[16,3584]{1,0:T(8,128)(2,1)S(1)}, u32[]{:S(2)}, u32[]{:S(2)}) collective-permute-start(bf16[16,3584]{1,0:T(8,128)(2,1)S(1)} %get-tuple-element.29), channel_id=1, source_target_pairs={{0,4},{1,5},{2,6},{3,7},{4,0},{5,1},{6,2},{7,3},{8,12},{9,13},{10,... | collective-permute-start | bytes 344072 | tf_op jit(solution)/shard_map/ppermute | solution.py:16
  73.7 4.8 %collective-permute-start.26 = (bf16[16,3584]{1,0:T(8,128)(2,1)S(1)}, bf16[16,3584]{1,0:T(8,128)(2,1)S(1)}, u32[]{:S(2)}, u32[]{:S(2)}) collective-permute-start(bf16[16,3584]{1,0:T(8,128)(2,1)S(1)} %get-tuple-element.31), channel_id=1, source_target_pairs={{0,8},{1,9},{2,10},{3,11},{4,12},{5,13},{6,14},{7,15},{8,0},{9,1},... | collective-permute-start | bytes 344072 | tf_op jit(solution)/shard_map/ppermute | solution.py:16
  74.0 4.8 %collective-permute-start.21 = (bf16[16,3584]{1,0:T(8,128)(2,1)S(1)}, bf16[16,3584]{1,0:T(8,128)(2,1)S(1)}, u32[]{:S(2)}, u32[]{:S(2)}) collective-permute-start(bf16[16,3584]{1,0:T(8,128)(2,1)S(1)} %get-tuple-element.27), channel_id=1, source_target_pairs={{0,2},{1,3},{2,0},{3,1},{4,6},{5,7},{6,4},{7,5},{8,10},{9,11},{10,... | collective-permute-start | bytes 344072 | tf_op jit(solution)/shard_map/ppermute | solution.py:16
  76.6 6.8 %collective-permute-start.30 = (bf16[16,3584]{1,0:T(8,128)(2,1)S(1)}, bf16[16,3584]{1,0:T(8,128)(2,1)S(1)}, u32[]{:S(2)}, u32[]{:S(2)}) collective-permute-start(bf16[16,3584]{1,0:T(8,128)(2,1)S(1)} %add_convert_fusion.1), channel_id=1, source_target_pairs={{0,16},{1,17},{2,18},{3,19},{4,20},{5,21},{6,22},{7,23},{8,24},{9,... | collective-permute-start | bytes 344072 | tf_op jit(solution)/shard_map/ppermute | solution.py:16
